TPU v7x, 32 devices: a whole 2x2x4 slice. The times are simulated.
32 devices in a mesh: fsdp: 4 (over z), ctx: 4 (over x, core), tp: 2 (over y).
Axes of the slice: x: 2, y: 2, z: 4, core: 2. Of those that a mesh axis runs over, the one named last changes fastest.
Arguments:
- tokens: bfloat16 [8, 4096, 1024], P('fsdp', ('ctx', 'tp')), may hold values from -6 to 6
- time_embed: float32 [8, 256], P('fsdp'), may hold values from -6 to 6
- segment_ids: int32 [8, 4096], P('fsdp'), may hold values from 0 to 15, as said below
- block_pairs: int32 [8, 4, 15, 2], P('fsdp', 'ctx'), may hold values from 0 to 7, as said below
- pair_counts: int32 [8, 4], P('fsdp', 'ctx'), may hold values from 2 to 15, as said below
- w_time: float32 [256, 2048], P(('fsdp', 'ctx')), may hold values from -0.1875 to 0.1875
- w_qkv: float32 [1024, 3072], P(('fsdp', 'ctx'), 'tp'), may hold values from -0.1875 to 0.1875
- w_out: float32 [1024, 1024], P(('fsdp', 'ctx'), 'tp'), may hold values from -1.5 to 1.5
- w_up: float32 [1024, 4096], P(('fsdp', 'ctx'), 'tp'), may hold values from -0.1875 to 0.1875
- w_down: float32 [1024, 4096], P(('fsdp', 'ctx'), 'tp'), may hold values from -0.09375 to 0.09375
- cotangent: bfloat16 [8, 4096, 1024], P('fsdp', ('ctx', 'tp')), may hold values from -6 to 6
Outputs:
- layer_out: bfloat16 [8, 4096, 1024], P('fsdp', ('ctx', 'tp'))
- grad_tokens: bfloat16 [8, 4096, 1024], P('fsdp', ('ctx', 'tp'))
- grad_time: float32 [256, 2048], P(('fsdp', 'ctx'))
- grad_qkv: float32 [1024, 3072], P(('fsdp', 'ctx'), 'tp')
- grad_proj: float32 [1024, 1024], P(('fsdp', 'ctx'), 'tp')
- grad_up: float32 [1024, 4096], P(('fsdp', 'ctx'), 'tp')
- grad_down: float32 [1024, 4096], P(('fsdp', 'ctx'), 'tp')
Inputs may be any that keep to these rules, and one draw needn't show every extreme that they name: `segment_ids`: in each row the ids start at 0 and never fall; a new document starts at a position with probability 1 / 512; row 0 holds one document; in the last row a document also starts at every multiple of 256 until the id reaches 15; ids stop rising at 15, so the last documents of a row may merge. `block_pairs`: for row r and ctx index c, slots p < pair_counts[r, c] list in increasing order of (local query block, key block) exactly the pairs of a local query block (0 to 1) and a key block of the row that share a document with the key not after the query; other slots hold 0. `pair_counts`: the number of listed pairs; the last ctx index of row 0 reaches 15.
All inputs are finite; a program needn't handle non-finite values.
Results may differ from a plain program's by a relative error of at most 0.02.
Values may be sent and summed in bfloat16 or wider, within the bound.
No kernel may reach another device: no remote copies, remote signals or barrier semaphores. Data moves between devices by JAX's collectives and lax.ppermute only.
A program may use at most 256 MiB of HBM per device.

v0:
```python
import functools

import jax
import jax.numpy as jnp
from jax import lax
from jax.experimental import pallas as pl
from jax.experimental.pallas import tpu as pltpu
from jax.sharding import Mesh
from jax.sharding import PartitionSpec as P

HEAD_DIM = 64
BLK = 512


epsilon = 1e-05
highest = lax.Precision.HIGHEST
masked_out = -1e30


def normalize(values):
    mean_value = jnp.mean(values, axis=-1, keepdims=True)
    centred = values - mean_value
    variance = jnp.mean(centred * centred, axis=-1, keepdims=True)
    inverse = lax.rsqrt(variance + epsilon)
    return (centred * inverse, inverse)


def normalize_back(grad_hat, normal_hat, inverse):
    first_mean = jnp.mean(grad_hat, axis=-1, keepdims=True)
    second_mean = jnp.mean(grad_hat * normal_hat, axis=-1, keepdims=True)
    return inverse * (grad_hat - first_mean - normal_hat * second_mean)


def smooth_gate(values):
    return jax.nn.gelu(values, approximate=True)


def block_scores(pair_entry, query_rows, key_rows, seg_row, offset):
    query_start = pair_entry[0] * BLK
    key_start = pair_entry[1] * BLK
    query_block = lax.dynamic_slice_in_dim(query_rows, query_start, BLK, 0)
    key_block = lax.dynamic_slice_in_dim(key_rows, key_start, BLK, 0)
    seg_query = lax.dynamic_slice_in_dim(seg_row, offset + query_start, BLK, 0)
    seg_keys = lax.dynamic_slice_in_dim(seg_row, key_start, BLK, 0)
    steps_in = jnp.arange(BLK, dtype=jnp.int32)
    allowed = (seg_query[:, None] == seg_keys[None, :]) & (
        key_start + steps_in[None, :] <= offset + query_start + steps_in[:, None]
    )
    scores = jnp.einsum(
        "qhe,khe->hqk", query_block, key_block, preferred_element_type=jnp.float32
    ) * HEAD_DIM ** (-0.5)
    return (query_block, key_block, query_start, key_start, allowed, scores)


def attend_forward(query_rows, key_rows, value_rows, seg_row, pair_rows, pair_total, offset):
    length_here, head_count, _ = query_rows.shape

    def statistic_step(pair_index, carried):
        running_max, running_sum = carried
        _, _, query_start, _, allowed, scores = block_scores(
            pair_rows[pair_index], query_rows, key_rows, seg_row, offset
        )
        scores = jnp.where(allowed[None], scores, masked_out)
        old_max = lax.dynamic_slice_in_dim(running_max, query_start, BLK, 1)
        old_sum = lax.dynamic_slice_in_dim(running_sum, query_start, BLK, 1)
        new_max = jnp.maximum(old_max, jnp.max(scores, axis=-1))
        weights = jnp.where(allowed[None], jnp.exp(scores - new_max[:, :, None]), 0.0)
        new_sum = old_sum * jnp.exp(old_max - new_max) + jnp.sum(weights, axis=-1)
        return (
            lax.dynamic_update_slice_in_dim(running_max, new_max, query_start, 1),
            lax.dynamic_update_slice_in_dim(running_sum, new_sum, query_start, 1),
        )

    start_max = jnp.full((head_count, length_here), masked_out, jnp.float32)
    start_sum = jnp.zeros((head_count, length_here), jnp.float32)
    running_max, running_sum = lax.fori_loop(0, pair_total, statistic_step, (start_max, start_sum))
    log_total = running_max + jnp.log(running_sum)

    def output_step(pair_index, accumulated):
        _, _, query_start, key_start, allowed, scores = block_scores(
            pair_rows[pair_index], query_rows, key_rows, seg_row, offset
        )
        block_log = lax.dynamic_slice_in_dim(log_total, query_start, BLK, 1)
        probabilities = jnp.where(
            allowed[None], jnp.exp(scores - block_log[:, :, None]), 0.0
        ).astype(jnp.bfloat16)
        value_block = lax.dynamic_slice_in_dim(value_rows, key_start, BLK, 0)
        addition = jnp.einsum(
            "hqk,khe->qhe", probabilities, value_block, preferred_element_type=jnp.float32
        )
        previous = lax.dynamic_slice_in_dim(accumulated, query_start, BLK, 0)
        return lax.dynamic_update_slice_in_dim(accumulated, previous + addition, query_start, 0)

    mixed_rows = lax.fori_loop(0, pair_total, output_step, jnp.zeros(query_rows.shape, jnp.float32))
    return (mixed_rows, log_total)


def attend_backward(
    query_rows,
    key_rows,
    value_rows,
    seg_row,
    pair_rows,
    pair_total,
    offset,
    log_total,
    grad_mixed,
    inner_sums,
):
    scale_factor = HEAD_DIM ** (-0.5)

    def add_block(whole, start_at, addition):
        previous = lax.dynamic_slice_in_dim(whole, start_at, BLK, 0)
        return lax.dynamic_update_slice_in_dim(whole, previous + addition, start_at, 0)

    def gradient_step(pair_index, carried):
        grad_query, grad_keys, grad_values = carried
        query_block, key_block, query_start, key_start, allowed, scores = block_scores(
            pair_rows[pair_index], query_rows, key_rows, seg_row, offset
        )
        block_log = lax.dynamic_slice_in_dim(log_total, query_start, BLK, 1)
        probabilities = jnp.where(allowed[None], jnp.exp(scores - block_log[:, :, None]), 0.0)
        grad_block = lax.dynamic_slice_in_dim(grad_mixed, query_start, BLK, 0)
        value_block = lax.dynamic_slice_in_dim(value_rows, key_start, BLK, 0)
        grad_probs = jnp.einsum(
            "qhe,khe->hqk", grad_block, value_block, preferred_element_type=jnp.float32
        )
        inner_block = lax.dynamic_slice_in_dim(inner_sums, query_start, BLK, 1)
        grad_scores = (probabilities * (grad_probs - inner_block[:, :, None])).astype(jnp.bfloat16)
        query_add = (
            jnp.einsum("hqk,khe->qhe", grad_scores, key_block, preferred_element_type=jnp.float32)
            * scale_factor
        )
        key_add = (
            jnp.einsum("hqk,qhe->khe", grad_scores, query_block, preferred_element_type=jnp.float32)
            * scale_factor
        )
        value_add = jnp.einsum(
            "hqk,qhe->khe",
            probabilities.astype(jnp.bfloat16),
            grad_block,
            preferred_element_type=jnp.float32,
        )
        return (
            add_block(grad_query, query_start, query_add),
            add_block(grad_keys, key_start, key_add),
            add_block(grad_values, key_start, value_add),
        )

    start_state = (
        jnp.zeros(query_rows.shape, jnp.float32),
        jnp.zeros(key_rows.shape, jnp.float32),
        jnp.zeros(value_rows.shape, jnp.float32),
    )
    return lax.fori_loop(0, pair_total, gradient_step, start_state)


def body(
    tokens,
    time_embed,
    segment_ids,
    block_pairs,
    pair_counts,
    w_time,
    w_qkv,
    w_out,
    w_up,
    w_down,
    cotangent,
):
    row_count, local_len, model_width = tokens.shape
    time_all, qkv_all, out_all, up_all, down_all = (
        lax.all_gather(w_time.astype(jnp.bfloat16), ("fsdp", "ctx"), axis=0, tiled=True),
        lax.all_gather(w_qkv.astype(jnp.bfloat16), ("fsdp", "ctx"), axis=0, tiled=True),
        lax.all_gather(w_out.astype(jnp.bfloat16), ("fsdp", "ctx"), axis=0, tiled=True),
        lax.all_gather(w_up.astype(jnp.bfloat16), ("fsdp", "ctx"), axis=0, tiled=True),
        lax.all_gather(w_down.astype(jnp.bfloat16), ("fsdp", "ctx"), axis=0, tiled=True),
    )
    scales = 1.0 + jnp.dot(time_embed, time_all.astype(jnp.float32), precision=highest)
    scale_attn = scales[:, None, :model_width]
    scale_mlp = scales[:, None, model_width:]
    x_input = tokens.astype(jnp.float32)
    hat_attn, inverse_attn = normalize(x_input)
    normed = (hat_attn * scale_attn).astype(jnp.bfloat16)
    normed_all = lax.all_gather(normed, "tp", axis=1, tiled=True)
    ctx_len = normed_all.shape[1]
    head_count = qkv_all.shape[1] // (3 * HEAD_DIM)
    projected = jnp.einsum("rtd,dc->rtc", normed_all, qkv_all, preferred_element_type=jnp.float32)
    projected = projected.astype(jnp.bfloat16).reshape(row_count, ctx_len, head_count, 3, HEAD_DIM)
    query_all = projected[:, :, :, 0]
    key_part = projected[:, :, :, 1]
    value_part = projected[:, :, :, 2]
    key_all, value_all = (
        lax.all_gather(key_part, "ctx", axis=1, tiled=True),
        lax.all_gather(value_part, "ctx", axis=1, tiled=True),
    )
    offset = lax.axis_index("ctx") * ctx_len
    mixed_list = []
    log_list = []
    for row_index in range(row_count):
        mixed_rows, log_total = attend_forward(
            query_all[row_index],
            key_all[row_index],
            value_all[row_index],
            segment_ids[row_index],
            block_pairs[row_index, 0],
            pair_counts[row_index, 0],
            offset,
        )
        mixed_list.append(mixed_rows)
        log_list.append(log_total)
    mixed_exact = jnp.stack(mixed_list)
    mixed_heads = mixed_exact.astype(jnp.bfloat16).reshape(
        row_count, ctx_len, head_count * HEAD_DIM
    )
    attn_part = jnp.einsum("rtc,dc->rtd", mixed_heads, out_all, preferred_element_type=jnp.float32)
    attn_local = lax.psum_scatter(
        attn_part.astype(jnp.bfloat16), "tp", scatter_dimension=1, tiled=True
    ).astype(jnp.float32)
    hidden = x_input + attn_local
    hat_mlp, inverse_mlp = normalize(hidden)
    normed_mlp = (hat_mlp * scale_mlp).astype(jnp.bfloat16)
    mlp_all = lax.all_gather(normed_mlp, "tp", axis=1, tiled=True)
    pre_act = jnp.einsum("rtd,df->rtf", mlp_all, up_all, preferred_element_type=jnp.float32)
    activated = smooth_gate(pre_act).astype(jnp.bfloat16)
    mlp_part = jnp.einsum("rtf,df->rtd", activated, down_all, preferred_element_type=jnp.float32)
    mlp_local = lax.psum_scatter(
        mlp_part.astype(jnp.bfloat16), "tp", scatter_dimension=1, tiled=True
    ).astype(jnp.float32)
    grad_all = lax.all_gather(cotangent, "tp", axis=1, tiled=True)
    grad_act = jnp.einsum("rtd,df->rtf", grad_all, down_all, preferred_element_type=jnp.float32)
    _, gate_back = jax.vjp(smooth_gate, pre_act)
    grad_pre = gate_back(grad_act)[0].astype(jnp.bfloat16)
    grad_down = jnp.einsum("rtd,rtf->df", grad_all, activated, preferred_element_type=jnp.float32)
    grad_up = jnp.einsum("rtd,rtf->df", mlp_all, grad_pre, preferred_element_type=jnp.float32)
    norm_part = jnp.einsum("rtf,df->rtd", grad_pre, up_all, preferred_element_type=jnp.float32)
    grad_normed_mlp = lax.psum_scatter(
        norm_part.astype(jnp.bfloat16), "tp", scatter_dimension=1, tiled=True
    ).astype(jnp.float32)
    layer_out = (hidden + mlp_local).astype(jnp.bfloat16)
    grad_output = cotangent.astype(jnp.float32)
    grad_scale_mlp = jnp.sum(grad_normed_mlp * hat_mlp, axis=1)
    grad_hidden = grad_output + normalize_back(grad_normed_mlp * scale_mlp, hat_mlp, inverse_mlp)
    grad_attn_all = lax.all_gather(grad_hidden.astype(jnp.bfloat16), "tp", axis=1, tiled=True)
    grad_mixed = jnp.einsum(
        "rtd,dc->rtc", grad_attn_all, out_all, preferred_element_type=jnp.float32
    ).astype(jnp.bfloat16)
    grad_proj = jnp.einsum(
        "rtd,rtc->dc", grad_attn_all, mixed_heads, preferred_element_type=jnp.float32
    )
    grad_mixed = grad_mixed.reshape(row_count, ctx_len, head_count, HEAD_DIM)
    inner_sums = jnp.einsum("rqhe,rqhe->rhq", grad_mixed.astype(jnp.float32), mixed_exact)
    query_grads = []
    key_grads = []
    value_grads = []
    for row_index in range(row_count):
        grad_query, grad_keys, grad_values = attend_backward(
            query_all[row_index],
            key_all[row_index],
            value_all[row_index],
            segment_ids[row_index],
            block_pairs[row_index, 0],
            pair_counts[row_index, 0],
            offset,
            log_list[row_index],
            grad_mixed[row_index],
            inner_sums[row_index],
        )
        query_grads.append(grad_query)
        key_grads.append(grad_keys)
        value_grads.append(grad_values)
    key_local, value_local = (
        lax.psum_scatter(
            jnp.stack(key_grads).astype(jnp.bfloat16), "ctx", scatter_dimension=1, tiled=True
        ).astype(jnp.float32),
        lax.psum_scatter(
            jnp.stack(value_grads).astype(jnp.bfloat16), "ctx", scatter_dimension=1, tiled=True
        ).astype(jnp.float32),
    )
    grad_projected = jnp.stack(
        [
            jnp.stack(query_grads).astype(jnp.bfloat16),
            key_local.astype(jnp.bfloat16),
            value_local.astype(jnp.bfloat16),
        ],
        axis=3,
    )
    grad_projected = grad_projected.reshape(row_count, ctx_len, head_count * 3 * HEAD_DIM)
    grad_qkv = jnp.einsum(
        "rtd,rtc->dc", normed_all, grad_projected, preferred_element_type=jnp.float32
    )
    first_part = jnp.einsum(
        "rtc,dc->rtd", grad_projected, qkv_all, preferred_element_type=jnp.float32
    )
    grad_normed = lax.psum_scatter(
        first_part.astype(jnp.bfloat16), "tp", scatter_dimension=1, tiled=True
    ).astype(jnp.float32)
    grad_scale_attn = jnp.sum(grad_normed * hat_attn, axis=1)
    grad_tokens = grad_hidden + normalize_back(grad_normed * scale_attn, hat_attn, inverse_attn)
    grad_scales = lax.psum(jnp.concatenate([grad_scale_attn, grad_scale_mlp], axis=1), "tp")
    grad_time = jnp.dot(time_embed.T, grad_scales, precision=highest)
    shared = (
        lax.psum_scatter(
            grad_time.astype(jnp.bfloat16), ("fsdp", "ctx"), scatter_dimension=0, tiled=True
        ).astype(jnp.float32),
        lax.psum_scatter(
            grad_qkv.astype(jnp.bfloat16), ("fsdp", "ctx"), scatter_dimension=0, tiled=True
        ).astype(jnp.float32),
        lax.psum_scatter(
            grad_proj.astype(jnp.bfloat16), ("fsdp", "ctx"), scatter_dimension=0, tiled=True
        ).astype(jnp.float32),
        lax.psum_scatter(
            grad_up.astype(jnp.bfloat16), ("fsdp", "ctx"), scatter_dimension=0, tiled=True
        ).astype(jnp.float32),
        lax.psum_scatter(
            grad_down.astype(jnp.bfloat16), ("fsdp", "ctx"), scatter_dimension=0, tiled=True
        ).astype(jnp.float32),
    )
    return (
        layer_out,
        grad_tokens.astype(jnp.bfloat16),
        shared[0],
        shared[1],
        shared[2],
        shared[3],
        shared[4],
    )


def params(limit=58):
    return pltpu.CompilerParams(vmem_limit_bytes=limit * 1024 * 1024)


def whole(shape):
    zeros = (0,) * len(shape)
    return pl.BlockSpec(shape, lambda *_: zeros, pipeline_mode=pl.Buffered(1))


def cost(flops, nbytes, exps=0):
    return pl.CostEstimate(flops=int(flops), bytes_accessed=int(nbytes), transcendentals=int(exps))


def dot_nn(left, right):
    return jnp.dot(left, right, preferred_element_type=jnp.float32)


def dot_nt(left, right):
    return lax.dot_general(left, right, (((1,), (1,)), ((), ())), preferred_element_type=jnp.float32)


def transposed(values):
    return values.astype(jnp.float32).T.astype(values.dtype)


def turned_apart(into_ref, values, core, chunks):
    turned = transposed(values)
    high = turned.shape[0] // chunks
    for chunk in range(chunks):
        inner = (chunk // 2 % 2) * (chunks // 4) + chunk // 4
        at = ((chunk % 2) ^ core) * (chunks // 2) + inner
        into_ref[pl.ds(pl.multiple_of(at * high, high), high), :] = turned[chunk * high : (chunk + 1) * high]


def put_apart(keep_ref, send_ref, grad):
    middle = grad.shape[0] // 2
    shape = (keep_ref.shape[0],) + keep_ref.shape[2:]
    keep_ref[:, 0] = grad[:middle].reshape(shape)
    send_ref[:, 0] = grad[middle:].reshape(shape)


def low_lanes(shape):
    return lax.broadcasted_iota(jnp.int32, shape, 1) < HEAD_DIM


def pair_apart(stored):
    first, second, third = stored[:, :128], stored[:, 128:256], stored[:, 256:]
    low = low_lanes(first.shape)
    keys = pltpu.roll(jnp.where(low, third, first), HEAD_DIM, 1)
    return jnp.concatenate(
        [jnp.where(low, first, second), keys, jnp.where(low, second, third)], axis=1
    )


def pair_together(query, keys, values):
    low = low_lanes(query.shape)
    turned = pltpu.roll(keys, HEAD_DIM, 1)
    return jnp.concatenate(
        [jnp.where(low, query, turned), jnp.where(low, values, query), jnp.where(low, turned, values)],
        axis=1,
    )


def project_kernel(place_ref, scales_ref, *refs, row, pieces, parts):
    weight_refs, token_refs = refs[:parts], refs[parts : parts + pieces]
    qkv_ref, normed_ref, held_ref, w_ref, sem_ref = refs[parts + pieces :]
    step = pl.program_id(0)

    def fetch(piece):
        source = token_refs[piece]
        source = source.at[row] if len(source.shape) == 3 else source
        return pltpu.make_async_copy(source, held_ref.at[piece], sem_ref.at[piece])

    @pl.when(step == 0)
    def _():
        for piece in range(pieces):
            fetch(piece).start()
        tall = weight_refs[0].shape[0]
        for apart, weight_ref in enumerate(weight_refs):
            at = pl.multiple_of((apart ^ place_ref[1]) * tall, tall)
            w_ref[pl.ds(at, tall), :] = pair_apart(weight_ref[...].astype(jnp.float32)).astype(jnp.bfloat16)
    pltpu.make_async_copy(held_ref.at[step], held_ref.at[step], sem_ref.at[step]).wait()
    values = held_ref[step].astype(jnp.float32)
    width = values.shape[1]
    hat, _ = normalize(values)
    normed = (hat * scales_ref[row : row + 1, :width]).astype(jnp.bfloat16)
    normed_ref[0] = normed
    qkv_ref[0] = dot_nn(normed, w_ref[...]).astype(jnp.bfloat16)


def project(row, place, scales, weights, tokens, others):
    _, length, width = tokens.shape
    pair = weights[0].shape[1]
    pieces = 1 + len(others)
    anywhere = pl.BlockSpec(memory_space=pl.ANY)
    return pl.pallas_call(
        functools.partial(project_kernel, row=row, pieces=pieces, parts=len(weights)),
        grid_spec=pltpu.PrefetchScalarGridSpec(
            num_scalar_prefetch=1,
            grid=(pieces,),
            in_specs=[whole(scales.shape)]
            + [whole(one.shape) for one in weights]
            + [anywhere] * pieces,
            out_specs=[
                pl.BlockSpec((1, length, pair), lambda i, place: (i ^ place[0], 0, 0)),
                pl.BlockSpec((1, length, width), lambda i, place: (i ^ place[0], 0, 0)),
            ],
            scratch_shapes=[
                pltpu.VMEM((pieces, length, width), jnp.bfloat16),
                pltpu.VMEM((width, pair), jnp.bfloat16),
                pltpu.SemaphoreType.DMA((pieces,)),
            ],
        ),
        out_shape=[
            jax.ShapeDtypeStruct((pieces, length, pair), jnp.bfloat16),
            jax.ShapeDtypeStruct((pieces, length, width), jnp.bfloat16),
        ],
        compiler_params=params(),
        cost_estimate=cost(2 * pieces * length * width * pair, 5 * pieces * length * width),
        name="project",
    )(place, scales, *weights, tokens, *others)


HALF = BLK // 2


def tile_mask(segc_ref, segr_ref, key_at, query_at, size):
    key_at, query_at = pl.multiple_of(key_at, size), pl.multiple_of(query_at, size)
    same = segc_ref[0, pl.ds(key_at, size), :] == segr_ref[0, :, pl.ds(query_at, size)]
    key_pos = key_at + lax.broadcasted_iota(jnp.int32, (size, size), 0)
    query_pos = query_at + lax.broadcasted_iota(jnp.int32, (size, size), 1)
    return same & (key_pos <= query_pos)


def split_heads(values):
    low = low_lanes(values.shape)
    zero = jnp.zeros_like(values)
    return jnp.concatenate([jnp.where(low, values, zero), jnp.where(low, zero, values)], axis=0)


def is_full(edge_ref, row, key_block, query_block):
    ends = edge_ref.shape[1] // 2
    same = edge_ref[row, 2 * key_block] == edge_ref[row, ends + 2 * query_block + 1]
    return same & (key_block < query_block)


def over_quarters(edge_ref, row, key_block, query_block, update):
    ends = edge_ref.shape[1] // 2

    def quarter(number, carried):
        key_half = 2 * key_block + number % 2
        query_half = 2 * query_block + number // 2
        shared = edge_ref[row, ends + key_half] >= edge_ref[row, query_half]

        @pl.when(shared & (key_half <= query_half))
        def _():
            update(pl.multiple_of(key_half * HALF, HALF), pl.multiple_of(query_half * HALF, HALF))

        return carried

    lax.fori_loop(0, 4, quarter, 0)


def largest(values, head):
    part = jnp.where(low_lanes(values.shape) == (head == 0), values, 0.0)
    return jnp.max(jnp.sum(part * part, axis=1, keepdims=True))


def attend_kernel(
    listed_ref, edge_ref, qkv_ref, segc_ref, segr_ref, mixed_ref, lse_ref,
    vt_ref, qz_ref, acc_ref, stat_ref, *, row,
):
    blocks = qkv_ref.shape[0]
    tall = HEAD_DIM + 16

    def turn(block, tops):
        at = pl.multiple_of(block * BLK, BLK)
        turned = transposed(qkv_ref[block, :, 256:384])
        ones = jnp.ones((16, BLK), jnp.bfloat16)
        for head in range(2):
            vt_ref[head * tall : head * tall + HEAD_DIM, pl.ds(at, BLK)] = turned[
                head * HEAD_DIM : (head + 1) * HEAD_DIM
            ]
            vt_ref[head * tall + HEAD_DIM : (head + 1) * tall, pl.ds(at, BLK)] = ones
        keys = qkv_ref[block, :, 128:256].astype(jnp.float32)
        return tuple(jnp.maximum(tops[head], largest(keys, head)) for head in range(2))

    key_tops = lax.fori_loop(0, blocks, turn, (0.0, 0.0))

    def one_query(query_block, carried):
        query = qkv_ref[query_block, :, :128].astype(jnp.float32) * HEAD_DIM ** (-0.5)
        qz_ref[...] = split_heads(query.astype(jnp.bfloat16))
        acc_ref[...] = jnp.zeros(acc_ref.shape, jnp.float32)
        shift = []
        for head in range(2):
            both = jnp.full((1, BLK), largest(query, head) * key_tops[head], jnp.float32)
            shift.append(jnp.sqrt(both) * 1.01)
        small = (jnp.max(shift[0]) < 40.0) & (jnp.max(shift[1]) < 40.0)

        def over_keys(full_update, part_update):
            def one_key(key_block, carried):
                listed = listed_ref[row, query_block * blocks + key_block] != 0
                full = is_full(edge_ref, row, key_block, query_block)

                @pl.when(listed & full)
                def _():
                    full_update(key_block)

                @pl.when(listed & jnp.logical_not(full))
                def _():
                    part_update(key_block)

                return carried

            lax.fori_loop(0, query_block + 1, one_key, 0)

        @pl.when(small)
        def _():
            def update(key_block, mask):
                at = pl.multiple_of(key_block * BLK, BLK)
                keys = qkv_ref[key_block, :, 128:256]
                parts = [slice(head * BLK, (head + 1) * BLK) for head in range(2)]
                scores = [dot_nt(keys, qz_ref[part, :]) for part in parts]
                for head, part in enumerate(parts):
                    one = scores[head] - shift[head]
                    if mask is not None:
                        one = jnp.where(mask, one, masked_out)
                    value = vt_ref[head * tall : (head + 1) * tall, pl.ds(at, BLK)]
                    acc_ref[:, part] += dot_nn(value, jnp.exp(one).astype(jnp.bfloat16))

            def part_update(key_block):
                update(key_block, tile_mask(segc_ref, segr_ref, key_block * BLK, query_block * BLK, BLK))

            def full_update(key_block):
                update(key_block, None)

            over_keys(full_update, part_update)
            stat_ref[0:1, :] = jnp.concatenate(shift, axis=1)

        @pl.when(jnp.logical_not(small))
        def _():
            stat_ref[0:1, :] = jnp.full((1, 2 * BLK), masked_out, jnp.float32)

            def part_update(key_at, query_at):
                keys = qkv_ref[key_at // BLK, pl.ds(pl.multiple_of(key_at % BLK, HALF), HALF), 128:256]
                mask = tile_mask(segc_ref, segr_ref, key_at, query_at, HALF)
                for head in range(2):
                    part = pl.ds(pl.multiple_of(head * BLK + query_at % BLK, HALF), HALF)
                    scores = jnp.where(mask, dot_nt(keys, qz_ref[part, :]), masked_out)
                    old_max = stat_ref[0:1, part]
                    new_max = jnp.maximum(old_max, jnp.max(scores, axis=0, keepdims=True))
                    weights = jnp.where(mask, jnp.exp(scores - new_max), 0.0)
                    value = vt_ref[head * tall : (head + 1) * tall, pl.ds(key_at, HALF)]
                    shrink = jnp.exp(old_max - new_max)
                    acc_ref[:, part] = acc_ref[:, part] * shrink + dot_nn(value, weights.astype(jnp.bfloat16))
                    stat_ref[0:1, part] = new_max

            def full_update(key_block):
                over_quarters(edge_ref, row, key_block, query_block, part_update)

            over_keys(full_update, full_update)

        total = acc_ref[HEAD_DIM : HEAD_DIM + 1, :]
        mixed = acc_ref[:HEAD_DIM, :] / total
        mixed = jnp.concatenate([mixed[:, :BLK], mixed[:, BLK:]], axis=0).T
        mixed_ref[query_block] = mixed.astype(jnp.bfloat16)
        log_total = stat_ref[0:1, :] + jnp.log(total)
        at = pl.multiple_of(query_block * BLK, BLK)
        lse_ref[0:1, pl.ds(at, BLK)] = log_total[:, :BLK]
        lse_ref[1:2, pl.ds(at, BLK)] = log_total[:, BLK:]
        return carried

    lax.fori_loop(0, blocks, one_query, 0)


def attend(row, listed, edges, qkv, segc, segr):
    blocks, blk, width = qkv.shape
    length = blocks * blk
    pair = 2 * HEAD_DIM
    return pl.pallas_call(
        functools.partial(attend_kernel, row=row),
        grid_spec=pltpu.PrefetchScalarGridSpec(
            num_scalar_prefetch=2,
            grid=(1,),
            in_specs=[
                whole(qkv.shape),
                pl.BlockSpec((1, length, 1), lambda i, *_: (row, 0, 0)),
                pl.BlockSpec((1, 1, length), lambda i, *_: (row, 0, 0)),
            ],
            out_specs=[whole((blocks, blk, pair)), whole((2, length))],
            scratch_shapes=[
                pltpu.VMEM((pair + 32, length), jnp.bfloat16),
                pltpu.VMEM((2 * blk, pair), jnp.bfloat16),
                pltpu.VMEM((HEAD_DIM + 16, 2 * blk), jnp.float32),
                pltpu.VMEM((1, 2 * blk), jnp.float32),
            ],
        ),
        out_shape=[
            jax.ShapeDtypeStruct((blocks, blk, pair), jnp.bfloat16),
            jax.ShapeDtypeStruct((2, length), jnp.float32),
        ],
        compiler_params=params(),
        cost_estimate=cost(20e9, 6e6, 20e6),
        name="attend",
    )(listed, edges, qkv, segc, segr)


def attend_back_kernel(
    listed_ref, edge_ref, qkv_ref, grad_ref, mixed_ref, lse_ref, segc_ref, segr_ref, out_ref,
    kt_ref, qz_ref, gz_ref, inner_ref, dq_ref, dk_ref, dv_ref, *, row,
):
    blocks = qkv_ref.shape[0]
    scale = HEAD_DIM ** (-0.5)

    def prepare(block, carried):
        at = pl.multiple_of(block * BLK, BLK)
        kt_ref[:, pl.ds(at, BLK)] = transposed(qkv_ref[block, :, 128:256])
        query = qkv_ref[block, :, :128].astype(jnp.float32) * scale
        qz_ref[block] = split_heads(query.astype(jnp.bfloat16))
        grad = grad_ref[block]
        gz_ref[block] = split_heads(grad)
        product = (grad.astype(jnp.float32) * mixed_ref[block].astype(jnp.float32)).T
        for head in range(2):
            part = product[head * HEAD_DIM : (head + 1) * HEAD_DIM, :]
            inner_ref[head : head + 1, pl.ds(at, BLK)] = jnp.sum(part, axis=0, keepdims=True)
        return carried

    lax.fori_loop(0, blocks, prepare, 0)
    dq_ref[...] = jnp.zeros(dq_ref.shape, jnp.float32)

    def one_key(key_block, carried):
        dk_ref[...] = jnp.zeros(dk_ref.shape, jnp.float32)
        dv_ref[...] = jnp.zeros(dv_ref.shape, jnp.float32)
        key_at = pl.multiple_of(key_block * BLK, BLK)

        def accumulate(head, key_at, query_at, keys, values, query, grad, mask):
            keys_here = pl.ds(pl.multiple_of(key_at % BLK, HALF), keys.shape[0])
            queries_here = pl.ds(query_at, query.shape[0])
            scores = dot_nt(keys, query)
            probs = jnp.exp(scores - lse_ref[head : head + 1, queries_here])
            if mask is not None:
                probs = jnp.where(mask, probs, 0.0)
            grad_probs = dot_nt(values, grad)
            grad_scores = probs * (grad_probs - inner_ref[head : head + 1, queries_here])
            probs = probs.astype(jnp.bfloat16)
            grad_scores = grad_scores.astype(jnp.bfloat16)
            dv_ref[keys_here, :] += dot_nn(probs, grad)
            dk_ref[keys_here, :] += dot_nn(grad_scores, query)
            lanes = slice(head * HEAD_DIM, (head + 1) * HEAD_DIM)
            dq_ref[lanes, queries_here] += dot_nn(
                kt_ref[lanes, pl.ds(key_at, keys.shape[0])], grad_scores
            )

        def full_update(query_block, mask):
            query_at = pl.multiple_of(query_block * BLK, BLK)
            keys = qkv_ref[key_block, :, 128:256]
            values = qkv_ref[key_block, :, 256:384]
            for head in range(2):
                part = slice(head * BLK, (head + 1) * BLK)
                query, grad = qz_ref[query_block, part, :], gz_ref[query_block, part, :]
                accumulate(head, key_at, query_at, keys, values, query, grad, mask)

        def one_query(query_block, carried):
            listed = listed_ref[row, query_block * blocks + key_block] != 0
            full = is_full(edge_ref, row, key_block, query_block)

            @pl.when(listed & full)
            def _():
                full_update(query_block, None)

            @pl.when(listed & jnp.logical_not(full))
            def _():
                full_update(query_block, tile_mask(segc_ref, segr_ref, key_block * BLK, query_block * BLK, BLK))

            return carried

        lax.fori_loop(key_block, blocks, one_query, 0)
        grad_query = dq_ref[:, pl.ds(key_at, BLK)].T * scale
        out_ref[key_block] = pair_together(grad_query, dk_ref[...], dv_ref[...]).astype(jnp.bfloat16)
        return carried

    lax.fori_loop(0, blocks, one_key, 0)


def attend_back(row, listed, edges, qkv, grad, mixed, lse, segc, segr):
    blocks, blk, width = qkv.shape
    length = blocks * blk
    pair = 2 * HEAD_DIM
    return pl.pallas_call(
        functools.partial(attend_back_kernel, row=row),
        grid_spec=pltpu.PrefetchScalarGridSpec(
            num_scalar_prefetch=2,
            grid=(1,),
            in_specs=[
                whole(qkv.shape),
                whole(grad.shape),
                whole(mixed.shape),
                whole(lse.shape),
                pl.BlockSpec((1, length, 1), lambda i, *_: (row, 0, 0)),
                pl.BlockSpec((1, 1, length), lambda i, *_: (row, 0, 0)),
            ],
            out_specs=whole(qkv.shape),
            scratch_shapes=[
                pltpu.VMEM((pair, length), jnp.bfloat16),
                pltpu.VMEM((blocks, 2 * blk, pair), jnp.bfloat16),
                pltpu.VMEM((blocks, 2 * blk, pair), jnp.bfloat16),
                pltpu.VMEM((2, length), jnp.float32),
                pltpu.VMEM((pair, length), jnp.float32),
                pltpu.VMEM((blk, pair), jnp.float32),
                pltpu.VMEM((blk, pair), jnp.float32),
            ],
        ),
        out_shape=jax.ShapeDtypeStruct(qkv.shape, jnp.bfloat16),
        compiler_params=params(),
        cost_estimate=cost(50e9, 10e6, 20e6),
        name="attend_back",
    )(listed, edges, qkv, grad, mixed, lse, segc, segr)


def joined(ref, half, halves):
    return jnp.concatenate([ref[i * halves + half] for i in range(ref.shape[0] // halves)], axis=1)


def outward_kernel(mixed_ref, tok_ref, w_ref, scales_ref, hidden_ref, normed_ref, *, row):
    halves = w_ref.shape[1]
    hidden = tok_ref[0].astype(jnp.float32)
    width = hidden.shape[1]
    for half in range(halves):
        hidden += dot_nt(joined(mixed_ref, half, halves), w_ref[:, half].reshape(width, -1))
    hidden_ref[...] = hidden
    hat, _ = normalize(hidden)
    normed_ref[...] = (hat * scales_ref[row : row + 1, width:]).astype(jnp.bfloat16)


def outward(row, mixed, tokens, w_all, scales, columns):
    rows, length, width = tokens.shape
    groups, _, pair = mixed.shape
    chunks, halves, high, _ = w_all.shape
    tile = 256
    one = pl.BlockSpec((tile, width), lambda i: (i, 0))
    return pl.pallas_call(
        functools.partial(outward_kernel, row=row),
        grid=(length // tile,),
        in_specs=[
            pl.BlockSpec((groups, tile, pair), lambda i: (0, i, 0)),
            pl.BlockSpec((1, tile, width), lambda i: (row, i, 0)),
            whole((chunks, halves, high, columns)),
            whole(scales.shape),
        ],
        out_specs=[one, one],
        out_shape=[
            jax.ShapeDtypeStruct((length, width), jnp.float32),
            jax.ShapeDtypeStruct((length, width), jnp.bfloat16),
        ],
        compiler_params=params(),
        cost_estimate=cost(2 * length * width * width, 12 * length * width),
        name="outward",
    )(mixed, tokens, w_all, scales)


def mlp_kernel(
    place_ref, nm0_ref, nm1_ref, cot_ref, hidden0_ref, hidden1_ref, scales_ref, up_ref, down_ref,
    keep_ref, send_ref, layer_ref, grad_hidden_ref, grad_attn_ref, gscale_ref,
    nmt_ref, cott_ref, out_ref, gn_ref, act_ref, gpre_ref,
):
    tile = pl.program_id(0)
    phase = pl.program_id(1)
    length, width = nm0_ref.shape
    count = 2 * length
    root = 0.7978845608028654
    cube = 0.044715

    @pl.when((tile == 0) & (phase == 0))
    def _():
        chunks = up_ref.shape[0]
        turned_apart(nmt_ref.at[:, :length], nm0_ref[...], place_ref[2], chunks)
        turned_apart(nmt_ref.at[:, length:], nm1_ref[...], place_ref[2], chunks)
        turned_apart(cott_ref, cot_ref[...], place_ref[2], chunks)
        out_ref[...] = jnp.zeros(out_ref.shape, jnp.float32)
        gn_ref[...] = jnp.zeros(gn_ref.shape, jnp.float32)

    @pl.when(phase == 0)
    def _():
        up = up_ref[:, 0].reshape(width, -1)
        down = down_ref[:, 0].reshape(width, -1)
        for row, nm_ref in enumerate((nm0_ref, nm1_ref)):
            part = slice(row * length, (row + 1) * length)
            pre = dot_nn(nm_ref[...], up)
            grad_act = dot_nn(cot_ref[part, :], down)
            square = pre * pre
            bent = jnp.tanh(root * (pre + cube * pre * square))
            half = 0.5 * (1.0 + bent)
            act_ref[part, :] = (pre * half).astype(jnp.bfloat16)
            slope = half + (0.5 * root) * pre * (1.0 - bent * bent) * (1.0 + (3.0 * cube) * square)
            gpre_ref[part, :] = (grad_act * slope).astype(jnp.bfloat16)
        put_apart(keep_ref, send_ref, dot_nn(nmt_ref[...], gpre_ref[...]).astype(jnp.bfloat16))

    @pl.when(phase == 1)
    def _():
        up = up_ref[:, 0].reshape(width, -1)
        down = down_ref[:, 0].reshape(width, -1)
        out_ref[...] += dot_nt(act_ref[...], down)
        gn_ref[...] += dot_nt(gpre_ref[...], up)
        put_apart(keep_ref, send_ref, dot_nn(cott_ref[...], act_ref[...]).astype(jnp.bfloat16))

    @pl.when((tile == pl.num_programs(0) - 1) & (phase == 1))
    def _():
        chunk = 256
        for row, hidden_ref in enumerate((hidden0_ref, hidden1_ref)):
            scale = scales_ref[row : row + 1, width:]
            total = jnp.zeros((1, width), jnp.float32)
            for at in range(0, length, chunk):
                part = slice(row * length + at, row * length + at + chunk)
                hidden = hidden_ref[at : at + chunk, :]
                layer_ref[part, :] = (hidden + out_ref[part, :]).astype(jnp.bfloat16)
                hat, inverse = normalize(hidden)
                grad = gn_ref[part, :]
                total += jnp.sum(grad * hat, axis=0, keepdims=True)
                back = cot_ref[part, :].astype(jnp.float32) + normalize_back(grad * scale, hat, inverse)
                grad_hidden_ref[part, :] = back
                grad_attn_ref[part, :] = back.astype(jnp.bfloat16)
            gscale_ref[row : row + 1, :] = total


def mlp(place, normed, cotangent, hidden, scales, w_all, room):
    rows, length, width = cotangent.shape
    count = rows * length
    chunks, halves, high, columns = w_all.shape
    tile = 512
    hidden_cols = (columns - room) // 2
    per_half = hidden_cols // tile
    first = room // tile
    flat = (count, width)
    one = (length, width)
    block = (chunks, 1, high, tile)
    apart = pl.BlockSpec(
        (2, 1, chunks // 4, high, tile),
        lambda f, s, at: (0, f // per_half, 0, 0, first + s * per_half + f % per_half),
    )
    grads = jax.ShapeDtypeStruct((2, halves, chunks // 4, high, columns), jnp.bfloat16)
    return pl.pallas_call(
        mlp_kernel,
        grid_spec=pltpu.PrefetchScalarGridSpec(
            num_scalar_prefetch=1,
            grid=(halves * per_half, 2),
            in_specs=[
                whole(one),
                whole(one),
                whole(flat),
                whole(one),
                whole(one),
                whole(scales.shape),
                pl.BlockSpec(block, lambda f, s, at: (0, f // per_half, 0, first + f % per_half)),
                pl.BlockSpec(block, lambda f, s, at: (0, f // per_half, 0, first + per_half + f % per_half)),
            ],
            out_specs=[
                apart,
                apart,
                whole(flat),
                whole(flat),
                whole(flat),
                whole((rows, width)),
            ],
            scratch_shapes=[
                pltpu.VMEM((width, count), jnp.bfloat16),
                pltpu.VMEM((width, count), jnp.bfloat16),
                pltpu.VMEM(flat, jnp.float32),
                pltpu.VMEM(flat, jnp.float32),
                pltpu.VMEM((count, tile), jnp.bfloat16),
                pltpu.VMEM((count, tile), jnp.bfloat16),
            ],
        ),
        out_shape=[
            grads,
            grads,
            jax.ShapeDtypeStruct(flat, jnp.bfloat16),
            jax.ShapeDtypeStruct(flat, jnp.float32),
            jax.ShapeDtypeStruct(flat, jnp.bfloat16),
            jax.ShapeDtypeStruct((rows, width), jnp.float32),
        ],
        compiler_params=params(60),
        cost_estimate=cost(12 * count * width * halves * hidden_cols, 4 * w_all.size + 16 * count * width),
        name="mlp",
    )(place, *normed, cotangent.reshape(flat), *hidden, scales, w_all, w_all)


def grad_mixed_kernel(grad_ref, w_ref, out_ref):
    halves = w_ref.shape[1]
    per_half = out_ref.shape[0] // halves
    grad = grad_ref[...]
    pair = out_ref.shape[2]
    for half in range(halves):
        out = dot_nn(grad, w_ref[:, half].reshape(grad.shape[1], -1)).astype(jnp.bfloat16)
        for group in range(per_half):
            out_ref[group * halves + half] = out[:, group * pair : (group + 1) * pair]


def grad_mixed_of(row, grad_attn, w_all, mixed_shape, columns):
    groups, length, pair = mixed_shape
    chunks, halves, high, _ = w_all.shape
    width = grad_attn.shape[1]
    tile = 256
    tiles = length // tile
    return pl.pallas_call(
        grad_mixed_kernel,
        grid=(tiles,),
        in_specs=[
            pl.BlockSpec((tile, width), lambda i: (row * tiles + i, 0)),
            whole((chunks, halves, high, columns)),
        ],
        out_specs=pl.BlockSpec((groups, tile, pair), lambda i: (0, i, 0)),
        out_shape=jax.ShapeDtypeStruct(mixed_shape, jnp.bfloat16),
        compiler_params=params(),
        cost_estimate=cost(2 * length * width * width, 8 * length * width),
        name="grad_mixed",
    )(grad_attn, w_all)


def grad_proj_kernel(place_ref, grad_ref, mixed0_ref, mixed1_ref, _k, _s, keep_ref, send_ref, turned_ref):
    half = pl.program_id(0)
    halves = pl.num_programs(0)

    @pl.when(half == 0)
    def _():
        turned_apart(turned_ref, grad_ref[...], place_ref[2], 4 * keep_ref.shape[2])

    groups, length, pair = mixed0_ref.shape
    count = keep_ref.shape[4] // pair
    grad = 0.0
    for row, mixed_ref in enumerate((mixed0_ref, mixed1_ref)):
        mixed = jnp.concatenate([mixed_ref[i * halves + half] for i in range(count)], axis=1)
        grad += dot_nn(turned_ref[:, row * length : (row + 1) * length], mixed)
    put_apart(keep_ref, send_ref, grad.astype(jnp.bfloat16))


def grad_proj_into(place, keep, send, grad_attn, mixed, columns):
    count, width = grad_attn.shape
    given = whole(mixed[0].shape)
    anywhere = pl.BlockSpec(memory_space=pl.ANY)
    out = pl.BlockSpec((2, 1) + keep.shape[2:4] + (columns,), lambda h, at: (0, h, 0, 0, 0))
    return pl.pallas_call(
        grad_proj_kernel,
        grid_spec=pltpu.PrefetchScalarGridSpec(
            num_scalar_prefetch=1,
            grid=(keep.shape[1],),
            in_specs=[whole(grad_attn.shape), given, given, anywhere, anywhere],
            out_specs=[out, out],
            scratch_shapes=[pltpu.VMEM((width, count), jnp.bfloat16)],
        ),
        out_shape=[jax.ShapeDtypeStruct(keep.shape, jnp.bfloat16)] * 2,
        input_output_aliases={4: 0, 5: 1},
        compiler_params=params(),
        cost_estimate=cost(2 * count * width * width, 6 * count * width),
        name="grad_proj",
    )(place, grad_attn, *mixed, keep, send)


def first_norm_kernel(gq_ref, tok_ref, grad_hidden_ref, w_ref, scales_ref, out_ref, gscale_ref, *, row, q_cols):
    step = pl.program_id(0)
    halves = w_ref.shape[1]
    values = tok_ref[0].astype(jnp.float32)
    width = values.shape[1]
    grad = jnp.zeros(values.shape, jnp.float32)
    for half in range(halves):
        weights = w_ref[:, half, :, :q_cols].reshape(width, q_cols)
        grad += dot_nt(joined(gq_ref, half, halves), weights)
    hat, inverse = normalize(values)
    total = jnp.sum(grad * hat, axis=0, keepdims=True)

    @pl.when(step == 0)
    def _():
        gscale_ref[...] = total

    @pl.when(step != 0)
    def _():
        gscale_ref[...] += total

    back = normalize_back(grad * scales_ref[row : row + 1, :width], hat, inverse)
    out_ref[...] = (grad_hidden_ref[...] + back).astype(jnp.bfloat16)


def first_norm_back(row, grad_qkv, tokens, grad_hidden, w_all, scales, q_cols):
    rows, length, width = tokens.shape
    groups, _, pair = grad_qkv.shape
    tile = 256
    tiles = length // tile
    return pl.pallas_call(
        functools.partial(first_norm_kernel, row=row, q_cols=q_cols),
        grid=(tiles,),
        in_specs=[
            pl.BlockSpec((groups, tile, pair), lambda i: (0, i, 0)),
            pl.BlockSpec((1, tile, width), lambda i: (row, i, 0)),
            pl.BlockSpec((tile, width), lambda i: (row * tiles + i, 0)),
            whole(w_all.shape),
            whole(scales.shape),
        ],
        out_specs=[pl.BlockSpec((tile, width), lambda i: (i, 0)), whole((1, width))],
        out_shape=[
            jax.ShapeDtypeStruct((length, width), jnp.bfloat16),
            jax.ShapeDtypeStruct((1, width), jnp.float32),
        ],
        compiler_params=params(),
        cost_estimate=cost(2 * length * width * groups * pair, 2 * w_all.size + 20 * length * width),
        name="first_norm_back",
    )(grad_qkv, tokens, grad_hidden, w_all, scales)


def grad_qkv_kernel(place_ref, normed_ref, gq_ref, *refs):
    step = pl.program_id(0)
    base_refs, out_refs, total_ref = refs[:-2], refs[-2:-1], refs[-1]
    if len(refs) > 3:
        base_refs, out_refs, (total_ref, turned_ref) = refs[:1], refs[1:-2], refs[-2:]

    @pl.when(step == 0)
    def _():
        total_ref[...] = base_refs[0][...] if base_refs else jnp.zeros(total_ref.shape, jnp.float32)

    total_ref[...] += dot_nn(transposed(gq_ref[0]), normed_ref[0])

    @pl.when(step == pl.num_programs(0) - 1)
    def _():
        if base_refs:
            turned_ref[...] = total_ref[...].T
            tall = out_refs[0].shape[0]
            for apart, out_ref in enumerate(out_refs):
                at = pl.multiple_of((apart ^ place_ref[1]) * tall, tall)
                out_ref[...] = turned_ref[pl.ds(at, tall), :].astype(jnp.bfloat16)
        else:
            out_refs[0][...] = total_ref[...]


def grad_qkv_of(place, normed, grad_qkv, parts, base=()):
    blocks, length, width = normed.shape
    pair = grad_qkv.shape[2]
    turned = (pair, width)
    if base:
        shapes = [jax.ShapeDtypeStruct((width // parts, pair), jnp.bfloat16)] * parts
    else:
        shapes = [jax.ShapeDtypeStruct(turned, jnp.float32)]
    return pl.pallas_call(
        grad_qkv_kernel,
        grid_spec=pltpu.PrefetchScalarGridSpec(
            num_scalar_prefetch=1,
            grid=(blocks,),
            in_specs=[
                pl.BlockSpec((1, length, width), lambda i, place: (i, 0, 0)),
                pl.BlockSpec((1, length, pair), lambda i, place: (i, 0, 0)),
            ]
            + [whole(turned)] * len(base),
            out_specs=[whole(one.shape) for one in shapes],
            scratch_shapes=[pltpu.VMEM(turned, jnp.float32)]
            + [pltpu.VMEM((width, pair), jnp.float32)] * len(base),
        ),
        out_shape=shapes,
        compiler_params=params(),
        cost_estimate=cost(2 * blocks * length * width * pair, 3 * blocks * length * width),
        name="grad_qkv",
    )(place, normed, grad_qkv, *base)


CTX = ("x", "core")
GROUP = ("x", "core", "tp")
EVERY = ("fsdp", "x", "core", "tp")


def size_of(axis):
    names = (axis,) if isinstance(axis, str) else axis
    return functools.reduce(lambda size, name: size * lax.axis_size(name), names, 1)


def across(values, axis, apart):
    size = size_of(axis)
    return lax.ppermute(values, axis, [(i, i ^ apart) for i in range(size)])


def summed(parts):
    return sum(part.astype(jnp.float32) for part in parts)


def exchange(values, axes):
    return lax.all_to_all(values, axes, 0, 0, tiled=True)


HOPS = {1: "tp", 2: "core", 4: "x"}


def widened(found, apart):
    return {**found, **{held ^ apart: across(one, HOPS[apart], 1) for held, one in found.items()}}


def listed_table(block_pairs, pair_counts, row_blocks, ctx_size):
    rows, _, slots, _ = block_pairs.shape
    packed = jnp.concatenate([block_pairs.reshape(rows, 1, slots * 2), pair_counts[:, :, None]], axis=2)
    packed = jnp.concatenate(
        [packed] + [across(packed, CTX, apart) for apart in range(1, ctx_size)], axis=1
    )
    pairs = packed[:, :, : slots * 2].reshape(rows, ctx_size, slots, 2)
    live = jnp.arange(slots, dtype=jnp.int32)[None, None, :] < packed[:, :, slots * 2 :]
    owner = lax.axis_index(CTX) ^ jnp.arange(ctx_size, dtype=jnp.int32)[None, :, None]
    base = owner * (row_blocks // ctx_size)
    code = jnp.where(live, (base + pairs[..., 0]) * row_blocks + pairs[..., 1], -1)
    code = code.reshape(rows, ctx_size * slots)
    cells = jnp.arange(row_blocks * row_blocks, dtype=jnp.int32)
    return jnp.any(code[:, :, None] == cells[None, None, :], axis=1).astype(jnp.int32)


def spread_body(
    tokens, time_embed, segment_ids, block_pairs, pair_counts,
    w_time, w_qkv, w_out, w_up, w_down, cotangent,
):
    rows, length, width = tokens.shape
    chunks = width // w_qkv.shape[0]
    halves = lax.axis_size("tp")
    high = w_qkv.shape[0]
    q_cols, o_cols, f_cols = w_qkv.shape[1], w_out.shape[1], w_up.shape[1]
    k_rows = w_time.shape[0]
    mine = lax.axis_index("tp")
    ctx, fsdp = lax.axis_index(CTX), lax.axis_index("fsdp")
    n_ctx, n_fsdp = size_of(CTX), lax.axis_size("fsdp")
    bf16, f32 = jnp.bfloat16, jnp.float32
    chunk = fsdp * n_ctx + ctx
    place = jnp.stack([ctx * halves + mine, fsdp, lax.axis_index("core")])

    found = [{0: tokens[row]} for row in range(rows)]
    orders = [(4, 1, 2) if row % 2 == 0 else (1, 4, 2) for row in range(rows)]
    found = [widened(one, order[0]) for one, order in zip(found, orders)]
    w_qkv = w_qkv.astype(bf16)
    columns = exchange(w_qkv.reshape(high, n_ctx, -1).transpose(1, 0, 2), CTX)
    embeds = [time_embed] + [across(time_embed, "fsdp", apart) for apart in range(1, n_fsdp)]
    w_time = w_time.astype(bf16)
    times = [w_time] + [across(w_time, CTX, apart) for apart in range(1, n_ctx)]
    row_blocks = segment_ids.shape[1] // BLK
    listed = listed_table(block_pairs, pair_counts, row_blocks, n_ctx)
    edges = jnp.concatenate([segment_ids[:, ::HALF], segment_ids[:, HALF - 1 :: HALF]], axis=1)
    segc = segment_ids[:, :, None]
    segr = segment_ids[:, None, :]
    second = jnp.concatenate([w_out, w_up, w_down], axis=1).astype(bf16)
    found, columns, embeds, times, second = lax.optimization_barrier((found, columns, embeds, times, second))
    second = lax.all_gather(second, EVERY, axis=0, tiled=True)
    found = [widened(one, order[1]) for one, order in zip(found, orders)]
    columns = columns.reshape(n_ctx * high, -1)
    columns = [columns] + [across(columns, "fsdp", apart) for apart in range(1, n_fsdp)]
    rows_of = [(chunk ^ apart) * k_rows for apart in range(n_ctx)]
    some = [
        jnp.concatenate([lax.dynamic_slice_in_dim(one, at, k_rows, 1) for at in rows_of], axis=1)
        for one in embeds
    ]
    mine_of = [one[:, :k_rows] for one in some]
    given = jnp.dot(jnp.concatenate(some, axis=0), jnp.concatenate(times, axis=0).astype(f32), precision=highest)
    given = given.reshape(n_fsdp, rows, -1)
    scales = 1.0 + given[0] + sum(across(given[apart], "fsdp", apart) for apart in range(1, n_fsdp))
    found, scales, columns, listed, edges, segc, segr = lax.optimization_barrier(
        (found, scales, columns, listed, edges, segc, segr)
    )
    found = [widened(one, order[2]) for one, order in zip(found, orders)]
    others = [[one[apart] for apart in range(1, len(one))] for one in found]

    qkv, normed = [], []
    for row in range(rows):
        out, one = project(row, place, scales, columns, tokens, others[row])
        qkv.append(out)
        normed.append(one)
    mixed_own, lse, mixed = [], [], []
    for row in range(rows):
        out, one = attend(row, listed, edges, qkv[row], segc, segr)
        mixed_own.append(out)
        lse.append(one)
        mixed.append(exchange(out, GROUP))
    mixed[0], mixed_own = lax.optimization_barrier((mixed[0], mixed_own))
    second = second.reshape(chunks, halves, high, -1)
    hidden, normed_mlp = [], []
    for row in range(rows):
        if row:
            mixed[row], hidden[row - 1] = lax.optimization_barrier((mixed[row], hidden[row - 1]))
        out, one = outward(row, mixed[row], tokens, second, scales, o_cols)
        hidden.append(out)
        normed_mlp.append(one)
    w_qkv, normed_mlp = lax.optimization_barrier((w_qkv, normed_mlp))
    third = lax.all_gather(w_qkv, EVERY, axis=0, tiled=True).reshape(chunks, halves, high, -1)
    keep, send, layer_out, grad_hidden, grad_attn, gscale_mlp = mlp(
        place, normed_mlp, cotangent, hidden, scales, second, o_cols
    )
    keep, send = grad_proj_into(place, keep, send, grad_attn, mixed, o_cols)
    grad_attn, keep, send, third = lax.optimization_barrier((grad_attn, keep, send, third))
    sent = across(send, "core", 1)
    grad_mixed = {}
    for row in reversed(range(rows)):
        out = grad_mixed_of(row, grad_attn, second, mixed[row].shape, o_cols)
        grad_mixed[row] = exchange(out, GROUP)
    last = rows - 1
    grads = summed([keep, sent]).astype(bf16)
    grad_mixed[last], grads = lax.optimization_barrier((grad_mixed[last], grads))
    grads = lax.psum_scatter(
        grads.reshape(-1, grads.shape[4]), ("x", "tp"), scatter_dimension=0, tiled=True
    )
    own, grad_qkv = {}, {}
    for row in reversed(range(rows)):
        if row < last:
            grad_mixed[row], own[row + 1] = lax.optimization_barrier((grad_mixed[row], own[row + 1]))
        own[row] = attend_back(row, listed, edges, qkv[row], grad_mixed[row], mixed_own[row], lse[row], segc, segr)
        if row < last:
            grad_qkv[row + 1] = exchange(own[row + 1], GROUP)
    grad_qkv[0] = exchange(own[0], GROUP)
    held, _ = lax.optimization_barrier((own[last], own[0]))
    base = grad_qkv_of(place, normed[last], held, n_fsdp)
    cut = list(grad_qkv_of(place, normed[0], own[0], n_fsdp, base))
    grad_tokens, gscale_attn = {}, {}
    held, _ = lax.optimization_barrier((grad_qkv[last], cut[0]))
    grad_tokens[last], gscale_attn[last] = first_norm_back(
        last, held, tokens, grad_hidden, third, scales, q_cols
    )
    cut[0], gscale_attn[last] = lax.optimization_barrier((cut[0], gscale_attn[last]))
    total = summed([cut[0]] + [across(cut[apart], "fsdp", apart) for apart in range(1, n_fsdp)])
    grads, gscale_attn[last], total = lax.optimization_barrier(
        (grads, gscale_attn[last], total.astype(bf16))
    )
    grads = lax.psum_scatter(grads, "fsdp", scatter_dimension=0, tiled=True)
    total = exchange(total.reshape(n_ctx, high, -1), CTX)
    grad_tokens[0], gscale_attn[0] = first_norm_back(
        0, grad_qkv[0], tokens, grad_hidden, third, scales, q_cols
    )
    devices = n_fsdp * n_ctx * halves
    both = jnp.concatenate([gscale_mlp, gscale_attn[last], gscale_attn[0]], axis=0)
    both = exchange(jnp.broadcast_to(both.astype(bf16)[None], (devices,) + both.shape), EVERY).astype(f32)
    both, total = lax.optimization_barrier((both, total))
    grad_w_qkv = total.transpose(1, 0, 2).reshape(high, q_cols).astype(f32)
    both = jnp.sum(both.reshape(n_fsdp, n_ctx * halves, 2 * rows, width), axis=1)
    both = jnp.concatenate([both[:, 3], both[:, 0], both[:, 2], both[:, 1]], axis=1)
    both = both.reshape(n_fsdp * rows, 2 * width)
    mine_of = [lax.dynamic_index_in_dim(jnp.stack(mine_of), i ^ fsdp, 0, False) for i in range(n_fsdp)]
    grad_time = jnp.dot(jnp.concatenate(mine_of, axis=0).T, both, precision=highest)
    return (
        layer_out.reshape(tokens.shape),
        jnp.stack([grad_tokens[row] for row in range(rows)]),
        grad_time,
        grad_w_qkv,
        grads[:, :o_cols].astype(f32),
        grads[:, o_cols : o_cols + f_cols].astype(f32),
        grads[:, o_cols + f_cols :].astype(f32),
    )


def specs_of(ctx):
    flat = ctx if isinstance(ctx, tuple) else (ctx,)
    tokens, weights = P("fsdp", (*flat, "tp"), None), P(("fsdp", *flat), "tp")
    placed = (tokens, P("fsdp", None), P("fsdp", None), P("fsdp", ctx, None, None), P("fsdp", ctx))
    placed += (P(("fsdp", *flat), None), weights, weights, weights, weights, tokens)
    return placed, (tokens, tokens, P(("fsdp", *flat), None), weights, weights, weights, weights)


def solution(mesh):
    sizes = tuple(mesh.shape[name] for name in ("fsdp", "ctx", "tp"))

    def run(*args):
        tokens, w_qkv, w_out, w_up = args[0], args[6], args[7], args[8]
        group = sizes[1] * sizes[2]
        fits = (
            sizes == (4, 4, 2)
            and tokens.shape[:2] == (8, group * BLK)
            and w_qkv.shape[1] == group * 6 * HEAD_DIM
            and w_out.shape[1] % (512 * sizes[2]) == 0
            and w_up.shape[1] % (512 * sizes[2]) == 0
        )
        if fits:
            devices = mesh.devices.reshape(sizes[0], 2, 2, sizes[2])
            parted = Mesh(devices, ("fsdp", "x", "core", "tp"))
            placed, given = specs_of(CTX)
            return jax.shard_map(
                spread_body, mesh=parted, in_specs=placed, out_specs=given, check_vma=False
            )(*args)
        placed, given = specs_of("ctx")
        return jax.shard_map(body, mesh=mesh, in_specs=placed, out_specs=given, check_vma=False)(*args)

    return run
```

profile of v0, /device:TPU:0, one launch (start us, length us, event | category | flops | bytes accessed | tf_op | source)
XLA Modules:
  0.0 588.9 jit_solution(12517684276046748051)
XLA Ops:
  7.2 1.8 slice_bitcast_fusion
  9.0 3.0 collective-permute-start
  12.0 1.5 collective-permute-start.1
  13.6 1.6 collective-permute-start.2
  15.1 2.6 collective-permute-start.3
  18.7 3.4 all-to-all-start
  22.1 1.5 convert_element_type.62
  25.2 1.7 collective-permute-start.6
  27.8 11.6 %collective-permute-done.6 = bf16[16,2048]{1,0:T(8,128)(2,1)S(1)} collective-permute-done((bf16[16,2048]{1,0:T(8,128)(2,1)}, bf16[16,2048]{1,0:T(8,128)(2,1)S(1)}, u32[]{:S(2)}, u32[]{:S(2)}) %collective-permute-start.6) | collective-permute-done | bytes 65568 | tf_op jit(solution)/shard_map/ppermute | solution.py:1102
  41.7 1.7 collective-permute-start.19
  46.6 1.1 fusion
  47.7 1.6 collective-permute-start.12
  49.4 2.6 collective-permute-start.13
  53.1 1.4 collective-permute-start.10
  55.1 1.5 collective-permute-start.8
  57.4 1.3 collective-permute-done.14
  59.4 11.5 %collective-permute-done.15.refs_1_ = bf16[256,384]{1,0:T(8,128)(2,1)S(1)} collective-permute-done((bf16[256,384]{1,0:T(8,128)(2,1)S(1)}, bf16[256,384]{1,0:T(8,128)(2,1)S(1)}, u32[]{:S(2)}, u32[]{:S(2)}) %collective-permute-start.15) | collective-permute-done | bytes 196640 | tf_op jit(solution)/shard_map/ppermute | solution.py:1102
  72.1 20.4 %collective-permute-done.16.refs_2_ = bf16[256,384]{1,0:T(8,128)(2,1)S(1)} collective-permute-done((bf16[256,384]{1,0:T(8,128)(2,1)S(1)}, bf16[256,384]{1,0:T(8,128)(2,1)S(1)}, u32[]{:S(2)}, u32[]{:S(2)}) %collective-permute-start.16) | collective-permute-done | bytes 196640 | tf_op jit(solution)/shard_map/ppermute | solution.py:1102
  92.6 2.2 collective-permute-start.17
  95.4 5.7 collective-permute-done.17.refs_3_
  101.1 17.6 %collective-permute-done.11.refs_9_ = bf16[512,1024]{1,0:T(8,128)(2,1)} collective-permute-done((bf16[512,1024]{1,0:T(8,128)(2,1)}, bf16[512,1024]{1,0:T(8,128)(2,1)}, u32[]{:S(2)}, u32[]{:S(2)}) %collective-permute-start.11) | collective-permute-done | bytes 1048608 | tf_op jit(solution)/shard_map/ppermute | solution.py:1102
  120.4 2.7 copy.83.segc_ref
  124.1 2.9 collective-permute-done.23.refs_10_
  127.1 2.1 collective-permute-done.24.refs_11_
  129.2 13.3 %project.2 = (bf16[8,512,384]{2,1,0:T(8,128)(2,1)}, bf16[8,512,1024]{2,1,0:T(8,128)(2,1)}) custom-call(s32[3]{0:T(128)} %pad_add_fusion.3.place_ref, f32[2,2048]{1,0:T(2,128)} %fusion.9.scales_ref, bf16[256,384]{1,0:T(8,128)(2,1)} %bitcast.77, bf16[256,384]{1,0:T(8,128)(2,1)} %copy-done.25, bf16[256,384]{1,0:T(8,128)(2,1)} %copy-done.26, ...), custom_call_target="tpu_custom_call" | custom-call | flops 3221225472 | bytes 20971520 | tf_op jit(solution)/shard_map/project/pallas_call | solution.py:425
  142.5 35.6 %attend.2 = (bf16[8,512,128]{2,1,0:T(8,128)(2,1)}, f32[2,4096]{1,0:T(2,128)}) custom-call(s32[2,64]{1,0:T(2,128)} %convert_element_type.63.listed_ref, s32[2,32]{1,0:T(2,128)} %pad_add_fusion.2.edge_ref, bf16[8,512,384]{2,1,0:T(8,128)(2,1)} %get-tuple-element.115.qkv_ref, s32[2,4096,1]{2,1,0:T(8,128)} %copy.83.segc_ref, s32[2,1,4096]{2,1,0:T(1,128)} %broadcast_in_dim.25.segr_ref), custom_call_target="tpu_custom_call" | custom-call | flops 20000000000 | bytes 6000000 | tf_op jit(solution)/shard_map/attend/pallas_call | solution.py:609
  178.1 3.8 all-to-all-start.1
  182.9 13.3 %project.3 = (bf16[8,512,384]{2,1,0:T(8,128)(2,1)}, bf16[8,512,1024]{2,1,0:T(8,128)(2,1)}) custom-call(s32[3]{0:T(128)} %pad_add_fusion.3.place_ref, f32[2,2048]{1,0:T(2,128)} %fusion.9.scales_ref, bf16[256,384]{1,0:T(8,128)(2,1)} %bitcast.78, bf16[256,384]{1,0:T(8,128)(2,1)} %copy-done.25, bf16[256,384]{1,0:T(8,128)(2,1)} %copy-done.26, ...), custom_call_target="tpu_custom_call" | custom-call | flops 3221225472 | bytes 20971520 | tf_op jit(solution)/shard_map/project/pallas_call | solution.py:425
  196.1 26.0 %attend.3 = (bf16[8,512,128]{2,1,0:T(8,128)(2,1)}, f32[2,4096]{1,0:T(2,128)}) custom-call(s32[2,64]{1,0:T(2,128)} %convert_element_type.63.listed_ref, s32[2,32]{1,0:T(2,128)} %pad_add_fusion.2.edge_ref, bf16[8,512,384]{2,1,0:T(8,128)(2,1)} %get-tuple-element.123.qkv_ref, s32[2,4096,1]{2,1,0:T(8,128)} %copy.83.segc_ref, s32[2,1,4096]{2,1,0:T(1,128)} %broadcast_in_dim.25.segr_ref), custom_call_target="tpu_custom_call" | custom-call | flops 20000000000 | bytes 6000000 | tf_op jit(solution)/shard_map/attend/pallas_call | solution.py:609
  222.1 4.3 all-to-all-start.2
  226.5 4.9 outward.2
  231.3 9.6 %all-to-all-done.2.mixed_ref.mixed1_ref = bf16[8,512,128]{2,1,0:T(8,128)(2,1)S(1)} async-done(((bf16[8,512,128]{2,1,0:T(8,128)(2,1)}), bf16[8,512,128]{2,1,0:T(8,128)(2,1)S(1)}, u32[]{:S(2)}, u32[]{:S(2)}) %all-to-all-start.2) | async-done | bytes 1048608 | tf_op jit(solution)/shard_map/all_to_all | solution.py:1110
  240.9 1.0 copy-done.2
  241.9 4.8 outward.3
  246.8 74.9 %mlp.1 = (bf16[2,2,4,64,4608]{4,3,2,1,0:T(8,128)(2,1)}, bf16[2,2,4,64,4608]{4,3,2,1,0:T(8,128)(2,1)}, bf16[1024,1024]{1,0:T(8,128)(2,1)}, f32[1024,1024]{1,0:T(8...) custom-call(s32[3]{0:T(128)} %pad_add_fusion.3.place_ref, bf16[512,1024]{1,0:T(8,128)(2,1)} %get-tuple-element.131.nm0_ref, ...), custom_call_target="tpu_custom_call" | custom-call | flops 51539607552 | bytes 54525952 | tf_op jit(solution)/shard_map/mlp/pallas_call | solution.py:870
  321.6 7.4 %grad_proj.1 = (bf16[2,2,4,64,4608]{4,3,2,1,0:T(8,128)(2,1)}, bf16[2,2,4,64,4608]{4,3,2,1,0:T(8,128)(2,1)}) custom-call(s32[3]{0:T(128)} %pad_add_fusion.3.place_ref, bf16[1024,1024]{1,0:T(8,128)(2,1)} %get-tuple-element.142.grad_ref, bf16[8,512,128]{2,1,0:T(8,128)(2,1)} %copy-done.1, ...), custom_call_target="tpu_custom_call", output_to_operand_aliasing={{0}: (4, {}), {1}: (5, {})} | custom-call | flops 2147483648 | bytes 6291456 | tf_op jit(solution)/shard_map/grad_proj/pallas_call | solution.py:970
  329.0 4.0 grad_mixed.3
  333.0 3.6 all-to-all-start.4
  336.7 7.4 %collective-permute-done.29 = bf16[2,2,4,64,4608]{4,3,2,1,0:T(8,128)(2,1)} collective-permute-done((bf16[2,2,4,64,4608]{4,3,2,1,0:T(8,128)(2,1)}, bf16[2,2,4,64,4608]{4,3,2,1,0:T(8,128)(2,1)}, u32[]{:S(2)}, u32[]{:S(2)}) %collective-permute-start.29) | collective-permute-done | bytes 9437216 | tf_op jit(solution)/shard_map/ppermute | solution.py:1102
  344.0 10.3 %add_convert_fusion = bf16[2,2,4,64,4608]{4,3,2,1,0:T(8,128)(2,1)} fusion(bf16[2,2,4,64,4608]{4,3,2,1,0:T(8,128)(2,1)} %collective-permute-done.29, bf16[2,2,4,64,4608]{4,3,2,1,0:T(8,128)(2,1)} %get-tuple-element.143), kind=kLoop, calls=%fused_computation | loop fusion | flops 18874368 | bytes 28311552 | tf_op jit(solution)/shard_map/convert_element_type | solution.py:1220
  354.4 0.9 copy-done.4
  355.3 4.0 grad_mixed.2
  359.3 3.6 all-to-all-start.3
  362.9 38.7 %attend_back.2.gq_ref = bf16[8,512,384]{2,1,0:T(8,128)(2,1)} custom-call(s32[2,64]{1,0:T(2,128)} %convert_element_type.63.listed_ref, s32[2,32]{1,0:T(2,128)} %pad_add_fusion.2.edge_ref, bf16[8,512,384]{2,1,0:T(8,128)(2,1)} %get-tuple-element.123.qkv_ref, bf16[8,512,128]{2,1,0:T(8,128)(2,1)} %copy-done.4, bf16[8,512,128]{2,1,0:T(8,128)(2,1)} %get-tuple-element.146.mixed_ref, ...), custom_call_target="tpu_custom_call" | custom-call | flops 49999998976 | bytes 10000000 | tf_op jit(solution)/shard_map/attend_back/pallas_call | solution.py:718
  401.6 1.0 copy-done.5
  402.6 4.1 all-to-all-start.6
  406.6 62.5 %attend_back.3.gq_ref = bf16[8,512,384]{2,1,0:T(8,128)(2,1)} custom-call(s32[2,64]{1,0:T(2,128)} %convert_element_type.63.listed_ref, s32[2,32]{1,0:T(2,128)} %pad_add_fusion.2.edge_ref, bf16[8,512,384]{2,1,0:T(8,128)(2,1)} %get-tuple-element.115.qkv_ref, bf16[8,512,128]{2,1,0:T(8,128)(2,1)} %copy-done.5, bf16[8,512,128]{2,1,0:T(8,128)(2,1)} %get-tuple-element.149.mixed_ref, ...), custom_call_target="tpu_custom_call" | custom-call | flops 49999998976 | bytes 10000000 | tf_op jit(solution)/shard_map/attend_back/pallas_call | solution.py:718
  469.1 11.0 %grad_qkv.2.refs_0_ = f32[384,1024]{1,0:T(8,128)} custom-call(s32[3]{0:T(128)} %pad_add_fusion.3.place_ref, bf16[8,512,1024]{2,1,0:T(8,128)(2,1)} %get-tuple-element.156.normed_ref, bf16[8,512,384]{2,1,0:T(8,128)(2,1)} %attend_back.2.gq_ref), custom_call_target="tpu_custom_call" | custom-call | flops 3221225472 | bytes 12582912 | tf_op jit(solution)/shard_map/grad_qkv/pallas_call | solution.py:1069
  480.1 11.8 %grad_qkv.3 = (bf16[256,384]{1,0:T(8,128)(2,1)}, bf16[256,384]{1,0:T(8,128)(2,1)}, bf16[256,384]{1,0:T(8,128)(2,1)}, bf16[256,384]{1,0:T(8,128)(2,1)}) custom-call(s32[3]{0:T(128)} %pad_add_fusion.3.place_ref, bf16[8,512,1024]{2,1,0:T(8,128)(2,1)} %get-tuple-element.155.normed_ref, bf16[8,512,384]{2,1,0:T(8,128)(2,1)} %attend_back.3.gq_ref, ...), custom_call_target="tpu_custom_call" | custom-call | flops 3221225472 | bytes 12582912 | tf_op jit(solution)/shard_map/grad_qkv/pallas_call | solution.py:1069
  491.9 4.3 collective-permute-start.32
  496.3 1.7 copy-done
  497.9 4.7 all-to-all-start.5
  502.6 9.2 %first_norm_back.3 = (bf16[512,1024]{1,0:T(8,128)(2,1)}, f32[1,1024]{1,0:T(1,128)}) custom-call(bf16[8,512,384]{2,1,0:T(8,128)(2,1)} %copy-done, bf16[2,512,1024]{2,1,0:T(8,128)(2,1)} %tok_ref.7, f32[1024,1024]{1,0:T(8,128)} %get-tuple-element.151.grad_hidden_ref, bf16[16,2,64,1536]{3,2,1,0:T(8,128)(2,1)} %bitcast.68, f32[2,2048]{1,0:T(2,128)} %fusion.9.scales_ref), custom_call_target="tpu_custom_call" | custom-call | flops 3221225472 | bytes 16777216 | tf_op jit(solution)/shard_map/first_norm_back/pallas_call | solution.py:1016
  511.9 1.7 add_convert_fusion.1
  513.7 25.9 %all-to-all-done.5.gq_ref = bf16[8,512,384]{2,1,0:T(8,128)(2,1)} async-done(((bf16[8,512,384]{2,1,0:T(8,128)(2,1)}), bf16[8,512,384]{2,1,0:T(8,128)(2,1)}, u32[]{:S(2)}, u32[]{:S(2)}) %all-to-all-start.5) | async-done | bytes 3145760 | tf_op jit(solution)/shard_map/all_to_all | solution.py:1110
  539.6 9.2 %first_norm_back.2 = (bf16[512,1024]{1,0:T(8,128)(2,1)}, f32[1,1024]{1,0:T(1,128)}) custom-call(bf16[8,512,384]{2,1,0:T(8,128)(2,1)} %all-to-all-done.5.gq_ref, bf16[2,512,1024]{2,1,0:T(8,128)(2,1)} %tok_ref.7, f32[1024,1024]{1,0:T(8,128)} %get-tuple-element.151.grad_hidden_ref, bf16[16,2,64,1536]{3,2,1,0:T(8,128)(2,1)} %bitcast.69, f32[2,2048]{1,0:T(2,128)} %fusion.9.scales_ref), custom_call_target="tpu_custom_call" | custom-call | flops 3221225472 | bytes 16777216 | tf_op jit(solution)/shard_map/first_norm_back/pallas_call | solution.py:1016
  550.3 2.6 all-to-all-start.7
  553.0 2.7 pad_maximum_fusion
  555.8 12.0 %all-to-all-done.7 = bf16[32,4,1024]{2,1,0:T(4,128)(2,1)S(1)} async-done(((bf16[32,4,1024]{2,1,0:T(4,128)(2,1)}), bf16[32,4,1024]{2,1,0:T(4,128)(2,1)S(1)}, u32[]{:S(2)}, u32[]{:S(2)}) %all-to-all-start.7) | async-done | bytes 262176 | tf_op jit(solution)/shard_map/all_to_all | solution.py:1110
  567.8 3.4 all-to-all-start.8
  571.3 5.2 all-to-all-done.8
  577.5 1.0 fusion.41
  578.5 2.1 slice_convert_fusion
  580.6 1.5 slice_convert_fusion.2
  (166 shorter events, 20.5 us)
Async XLA Ops:
  7.2 6.4 %copy-start.14 = (f32[2,256]{1,0:T(2,128)S(1)}, f32[2,256]{1,0:T(2,128)}, u32[]{:S(2)}) copy-start(f32[2,256]{1,0:T(2,128)} %param.12) | copy-start | bytes 6148
  7.2 10.8 %copy-start.9 = (f32[64,1536]{1,0:T(8,128)S(1)}, f32[64,1536]{1,0:T(8,128)}, u32[]{:S(2)}) copy-start(f32[64,1536]{1,0:T(8,128)} %param.17) | copy-start | bytes 1179652
  7.2 16.5 %copy-start.7 = (f32[64,2048]{1,0:T(8,128)S(1)}, f32[64,2048]{1,0:T(8,128)}, u32[]{:S(2)}) copy-start(f32[64,2048]{1,0:T(8,128)} %param.19) | copy-start | bytes 1572868
  7.2 16.5 %copy-start.8 = (f32[64,2048]{1,0:T(8,128)S(1)}, f32[64,2048]{1,0:T(8,128)}, u32[]{:S(2)}) copy-start(f32[64,2048]{1,0:T(8,128)} %param.20) | copy-start | bytes 1572868
  9.0 30.5 %collective-permute-start = (bf16[512,1024]{1,0:T(8,128)(2,1)S(1)}, bf16[512,1024]{1,0:T(8,128)(2,1)}, u32[]{:S(2)}, u32[]{:S(2)}) collective-permute-start(bf16[512,1024]{1,0:T(8,128)(2,1)S(1)} %get-tuple-element.112), channel_id=1, source_target_pairs={{0,4},{4,0},{1,5},{5,1},{2,6},{6,2},{3,7},{7,3},{8,12},{12,8},{9,1... | collective-permute-start | bytes 3145736 | tf_op jit(solution)/shard_map/ppermute | solution.py:1102
  12.0 27.4 %collective-permute-start.1 = (bf16[512,1024]{1,0:T(8,128)(2,1)S(1)}, bf16[512,1024]{1,0:T(8,128)(2,1)}, u32[]{:S(2)}, u32[]{:S(2)}) collective-permute-start(bf16[512,1024]{1,0:T(8,128)(2,1)S(1)} %get-tuple-element.120), channel_id=1, source_target_pairs={{0,1},{1,0},{2,3},{3,2},{4,5},{5,4},{6,7},{7,6},{8,9},{9,8},{10,11... | collective-permute-start | bytes 3145736 | tf_op jit(solution)/shard_map/ppermute | solution.py:1102
  13.6 11.1 %collective-permute-start.2 = (f32[2,256]{1,0:T(2,128)S(1)}, f32[2,256]{1,0:T(2,128)S(1)}, u32[]{:S(2)}, u32[]{:S(2)}) collective-permute-start(f32[2,256]{1,0:T(2,128)S(1)} %copy-done.14), channel_id=1, source_target_pairs={{0,8},{8,0},{16,24},{24,16},{1,9},{9,1},{17,25},{25,17},{2,10},{10... | collective-permute-start | bytes 6152 | tf_op jit(solution)/shard_map/ppermute | solution.py:1102
  15.1 10.1 %collective-permute-start.3 = (f32[2,256]{1,0:T(2,128)S(1)}, f32[2,256]{1,0:T(2,128)S(1)}, u32[]{:S(2)}, u32[]{:S(2)}) collective-permute-start(f32[2,256]{1,0:T(2,128)S(1)} %copy-done.14), channel_id=1, source_target_pairs={{0,16},{8,24},{16,0},{24,8},{1,17},{9,25},{17,1},{25,9},{2,18},{10... | collective-permute-start | bytes 6152 | tf_op jit(solution)/shard_map/ppermute | solution.py:1102
  17.7 9.2 %collective-permute-start.4 = (f32[2,256]{1,0:T(2,128)S(1)}, f32[2,256]{1,0:T(2,128)S(1)}, u32[]{:S(2)}, u32[]{:S(2)}) collective-permute-start(f32[2,256]{1,0:T(2,128)S(1)} %copy-done.14), channel_id=1, source_target_pairs={{0,24},{8,16},{16,8},{24,0},{1,25},{9,17},{17,9},{25,1},{2,26},{10... | collective-permute-start | bytes 6152 | tf_op jit(solution)/shard_map/ppermute | solution.py:1102
  18.0 105.1 %copy-start.3 = (bf16[64,1536]{1,0:T(8,128)(2,1)}, bf16[64,1536]{1,0:T(8,128)(2,1)S(1)}, u32[]{:S(2)}) copy-start(bf16[64,1536]{1,0:T(8,128)(2,1)S(1)} %convert_element_type.61) | copy-start | bytes 589828
  18.7 20.8 %all-to-all-start = ((bf16[4,64,384]{2,1,0:T(8,128)(2,1)}), bf16[4,64,384]{2,1,0:T(8,128)(2,1)S(1)}, u32[]{:S(2)}, u32[]{:S(2)}) async-start(bf16[4,64,384]{2,1,0:T(8,128)(2,1)} %bitcast.59), calls=%async_computation | async-start | bytes 393216 | tf_op jit(solution)/shard_map/all_to_all | solution.py:1110
  22.1 204.3 %all-gather.3.cloned.1.call-start = ((), (), s32[]{:S(2)}) async-start(), calls=%async_computation.11 | async-start | bytes 19464192 | tf_op jit(solution)/shard_map/all_gather | solution.py:1168
  23.7 28.3 %copy-start.12 = (s32[2,4096]{1,0:T(2,128)S(1)}, s32[2,4096]{1,0:T(2,128)}, u32[]{:S(2)}) copy-start(s32[2,4096]{1,0:T(2,128)} %param.13) | copy-start | bytes 98308
  24.7 3.1 collective-permute-start.5
  25.2 14.2 %collective-permute-start.6 = (bf16[16,2048]{1,0:T(8,128)(2,1)}, bf16[16,2048]{1,0:T(8,128)(2,1)S(1)}, u32[]{:S(2)}, u32[]{:S(2)}) collective-permute-start(bf16[16,2048]{1,0:T(8,128)(2,1)} %convert_element_type.62), channel_id=1, source_target_pairs={{0,4},{2,6},{4,0},{6,2},{1,5},{3,7},{5,1},{7,3},{8,12},{10,14},{12... | collective-permute-start | bytes 196616 | tf_op jit(solution)/shard_map/ppermute | solution.py:1102
  26.9 12.6 %collective-permute-start.7 = (bf16[16,2048]{1,0:T(8,128)(2,1)}, bf16[16,2048]{1,0:T(8,128)(2,1)S(1)}, u32[]{:S(2)}, u32[]{:S(2)}) collective-permute-start(bf16[16,2048]{1,0:T(8,128)(2,1)} %convert_element_type.62), channel_id=1, source_target_pairs={{0,6},{2,4},{4,2},{6,0},{1,7},{3,5},{5,3},{7,1},{8,14},{10,12},{12... | collective-permute-start | bytes 196616 | tf_op jit(solution)/shard_map/ppermute | solution.py:1102
  39.5 83.6 %copy-start.10 = (bf16[4,64,384]{2,1,0:T(8,128)(2,1)}, bf16[4,64,384]{2,1,0:T(8,128)(2,1)S(1)}, u32[]{:S(2)}) copy-start(bf16[4,64,384]{2,1,0:T(8,128)(2,1)S(1)} %all-to-all-done) | copy-start | bytes 589828
  41.2 11.6 %collective-permute-start.18 = (s32[2,1,31]{2,0,1:T(2,128)S(1)}, s32[2,1,31]{2,0,1:T(2,128)S(1)}, u32[]{:S(2)}, u32[]{:S(2)}) collective-permute-start(s32[2,1,31]{2,0,1:T(2,128)S(1)} %pad_add_fusion.1), channel_id=1, source_target_pairs={{0,2},{2,0},{4,6},{6,4},{1,3},{3,1},{5,7},{7,5},{8,10},{10,8},{12,... | collective-permute-start | bytes 752 | tf_op jit(solution)/shard_map/ppermute | solution.py:1102
  41.7 11.4 %collective-permute-start.19 = (s32[2,1,31]{2,0,1:T(2,128)S(1)}, s32[2,1,31]{2,0,1:T(2,128)S(1)}, u32[]{:S(2)}, u32[]{:S(2)}) collective-permute-start(s32[2,1,31]{2,0,1:T(2,128)S(1)} %pad_add_fusion.1), channel_id=1, source_target_pairs={{0,4},{2,6},{4,0},{6,2},{1,5},{3,7},{5,1},{7,3},{8,12},{10,14},{12... | collective-permute-start | bytes 752 | tf_op jit(solution)/shard_map/ppermute | solution.py:1102
  43.5 11.1 %collective-permute-start.20 = (s32[2,1,31]{2,0,1:T(2,128)S(1)}, s32[2,1,31]{2,0,1:T(2,128)S(1)}, u32[]{:S(2)}, u32[]{:S(2)}) collective-permute-start(s32[2,1,31]{2,0,1:T(2,128)S(1)} %pad_add_fusion.1), channel_id=1, source_target_pairs={{0,6},{2,4},{4,2},{6,0},{1,7},{3,5},{5,3},{7,1},{8,14},{10,12},{12... | collective-permute-start | bytes 752 | tf_op jit(solution)/shard_map/ppermute | solution.py:1102
  46.0 96.5 %copy-start.20 = (f32[2,16]{1,0:T(2,128)}, f32[2,16]{1,0:T(2,128)S(1)}, u32[]{:S(2)}) copy-start(f32[2,16]{1,0:T(2,128)S(1)} %get-tuple-element.204) | copy-start | bytes 388
  47.7 7.4 %collective-permute-start.12 = (f32[2,2048]{1,0:T(2,128)S(1)}, f32[2,2048]{1,0:T(2,128)S(1)}, u32[]{:S(2)}, u32[]{:S(2)}) collective-permute-start(f32[2,2048]{1,0:T(2,128)S(1)} %get-tuple-element.185), channel_id=1, source_target_pairs={{0,8},{8,0},{16,24},{24,16},{1,9},{9,1},{17,25},{25,17},{2,10},{10... | collective-permute-start | bytes 49160 | tf_op jit(solution)/shard_map/ppermute | solution.py:1102
  49.4 7.3 %collective-permute-start.13 = (f32[2,2048]{1,0:T(2,128)S(1)}, f32[2,2048]{1,0:T(2,128)S(1)}, u32[]{:S(2)}, u32[]{:S(2)}) collective-permute-start(f32[2,2048]{1,0:T(2,128)S(1)} %get-tuple-element.183), channel_id=1, source_target_pairs={{0,16},{8,24},{16,0},{24,8},{1,17},{9,25},{17,1},{25,9},{2,18},{10... | collective-permute-start | bytes 49160 | tf_op jit(solution)/shard_map/ppermute | solution.py:1102
  52.9 5.9 collective-permute-start.14
  53.1 48.0 %collective-permute-start.10 = (bf16[512,1024]{1,0:T(8,128)(2,1)S(1)}, bf16[512,1024]{1,0:T(8,128)(2,1)}, u32[]{:S(2)}, u32[]{:S(2)}) collective-permute-start(bf16[512,1024]{1,0:T(8,128)(2,1)S(1)} %get-tuple-element.120), channel_id=1, source_target_pairs={{0,4},{4,0},{1,5},{5,1},{2,6},{6,2},{3,7},{7,3},{8,12},{12,8},{9,1... | collective-permute-start | bytes 3145736 | tf_op jit(solution)/shard_map/ppermute | solution.py:1102
  54.5 64.2 %collective-permute-start.11 = (bf16[512,1024]{1,0:T(8,128)(2,1)}, bf16[512,1024]{1,0:T(8,128)(2,1)}, u32[]{:S(2)}, u32[]{:S(2)}) collective-permute-start(bf16[512,1024]{1,0:T(8,128)(2,1)} %collective-permute-done.1.refs_5_), channel_id=1, source_target_pairs={{0,4},{4,0},{1,5},{5,1},{2,6},{6,2},{3,7},{7,3},{8,12},{12,8},{9,1... | collective-permute-start | bytes 3145736 | tf_op jit(solution)/shard_map/ppermute | solution.py:1102
  55.1 63.6 %collective-permute-start.8 = (bf16[512,1024]{1,0:T(8,128)(2,1)S(1)}, bf16[512,1024]{1,0:T(8,128)(2,1)}, u32[]{:S(2)}, u32[]{:S(2)}) collective-permute-start(bf16[512,1024]{1,0:T(8,128)(2,1)S(1)} %get-tuple-element.112), channel_id=1, source_target_pairs={{0,1},{1,0},{2,3},{3,2},{4,5},{5,4},{6,7},{7,6},{8,9},{9,8},{10,11... | collective-permute-start | bytes 3145736 | tf_op jit(solution)/shard_map/ppermute | solution.py:1102
  56.7 62.1 %collective-permute-start.9 = (bf16[512,1024]{1,0:T(8,128)(2,1)}, bf16[512,1024]{1,0:T(8,128)(2,1)}, u32[]{:S(2)}, u32[]{:S(2)}) collective-permute-start(bf16[512,1024]{1,0:T(8,128)(2,1)} %collective-permute-done.refs_8_), channel_id=1, source_target_pairs={{0,1},{1,0},{2,3},{3,2},{4,5},{5,4},{6,7},{7,6},{8,9},{9,8},{10,11... | collective-permute-start | bytes 3145736 | tf_op jit(solution)/shard_map/ppermute | solution.py:1102
  58.7 12.1 %collective-permute-start.15 = (bf16[256,384]{1,0:T(8,128)(2,1)S(1)}, bf16[256,384]{1,0:T(8,128)(2,1)S(1)}, u32[]{:S(2)}, u32[]{:S(2)}) collective-permute-start(bf16[256,384]{1,0:T(8,128)(2,1)S(1)} %bitcast.74), channel_id=1, source_target_pairs={{0,8},{8,0},{16,24},{24,16},{1,9},{9,1},{17,25},{25,17},{2,10},{10... | collective-permute-start | bytes 589832 | tf_op jit(solution)/shard_map/ppermute | solution.py:1102
  70.9 58.3 %copy-start.25 = (bf16[256,384]{1,0:T(8,128)(2,1)}, bf16[256,384]{1,0:T(8,128)(2,1)S(1)}, u32[]{:S(2)}) copy-start(bf16[256,384]{1,0:T(8,128)(2,1)S(1)} %collective-permute-done.15.refs_1_) | copy-start | bytes 589828
  70.9 21.7 %collective-permute-start.16 = (bf16[256,384]{1,0:T(8,128)(2,1)S(1)}, bf16[256,384]{1,0:T(8,128)(2,1)S(1)}, u32[]{:S(2)}, u32[]{:S(2)}) collective-permute-start(bf16[256,384]{1,0:T(8,128)(2,1)S(1)} %bitcast.75), channel_id=1, source_target_pairs={{0,16},{8,24},{16,0},{24,8},{1,17},{9,25},{17,1},{25,9},{2,18},{10... | collective-permute-start | bytes 589832 | tf_op jit(solution)/shard_map/ppermute | solution.py:1102
  92.6 30.5 %copy-start.26 = (bf16[256,384]{1,0:T(8,128)(2,1)}, bf16[256,384]{1,0:T(8,128)(2,1)S(1)}, u32[]{:S(2)}) copy-start(bf16[256,384]{1,0:T(8,128)(2,1)S(1)} %collective-permute-done.16.refs_2_) | copy-start | bytes 589828
  92.6 8.5 %collective-permute-start.17 = (bf16[256,384]{1,0:T(8,128)(2,1)S(1)}, bf16[256,384]{1,0:T(8,128)(2,1)S(1)}, u32[]{:S(2)}, u32[]{:S(2)}) collective-permute-start(bf16[256,384]{1,0:T(8,128)(2,1)S(1)} %bitcast.76), channel_id=1, source_target_pairs={{0,24},{8,16},{16,8},{24,0},{1,25},{9,17},{17,9},{25,1},{2,26},{10... | collective-permute-start | bytes 589832 | tf_op jit(solution)/shard_map/ppermute | solution.py:1102
  101.1 22.0 %copy-start.27 = (bf16[256,384]{1,0:T(8,128)(2,1)}, bf16[256,384]{1,0:T(8,128)(2,1)S(1)}, u32[]{:S(2)}) copy-start(bf16[256,384]{1,0:T(8,128)(2,1)S(1)} %collective-permute-done.17.refs_3_) | copy-start | bytes 589828
  118.7 4.4 collective-permute-start.21
  118.7 5.2 collective-permute-start.22
  119.2 7.7 %collective-permute-start.23 = (bf16[512,1024]{1,0:T(8,128)(2,1)}, bf16[512,1024]{1,0:T(8,128)(2,1)}, u32[]{:S(2)}, u32[]{:S(2)}) collective-permute-start(bf16[512,1024]{1,0:T(8,128)(2,1)} %collective-permute-done.refs_8_), channel_id=1, source_target_pairs={{0,2},{2,0},{1,3},{3,1},{4,6},{6,4},{5,7},{7,5},{8,10},{10,8},{9,1... | collective-permute-start | bytes 3145736 | tf_op jit(solution)/shard_map/ppermute | solution.py:1102
  119.3 9.9 %collective-permute-start.24 = (bf16[512,1024]{1,0:T(8,128)(2,1)}, bf16[512,1024]{1,0:T(8,128)(2,1)}, u32[]{:S(2)}, u32[]{:S(2)}) collective-permute-start(bf16[512,1024]{1,0:T(8,128)(2,1)} %collective-permute-done.9.refs_9_), channel_id=1, source_target_pairs={{0,2},{2,0},{1,3},{3,1},{4,6},{6,4},{5,7},{7,5},{8,10},{10,8},{9,1... | collective-permute-start | bytes 3145736 | tf_op jit(solution)/shard_map/ppermute | solution.py:1102
  120.4 61.5 %collective-permute-start.25 = (bf16[512,1024]{1,0:T(8,128)(2,1)S(1)}, bf16[512,1024]{1,0:T(8,128)(2,1)}, u32[]{:S(2)}, u32[]{:S(2)}) collective-permute-start(bf16[512,1024]{1,0:T(8,128)(2,1)S(1)} %get-tuple-element.120), channel_id=1, source_target_pairs={{0,2},{2,0},{1,3},{3,1},{4,6},{6,4},{5,7},{7,5},{8,10},{10,8},{9,1... | collective-permute-start | bytes 3145736 | tf_op jit(solution)/shard_map/ppermute | solution.py:1102
  123.1 58.7 %collective-permute-start.26 = (bf16[512,1024]{1,0:T(8,128)(2,1)}, bf16[512,1024]{1,0:T(8,128)(2,1)S(1)}, u32[]{:S(2)}, u32[]{:S(2)}) collective-permute-start(bf16[512,1024]{1,0:T(8,128)(2,1)} %collective-permute-done.1.refs_5_), channel_id=1, source_target_pairs={{0,2},{2,0},{1,3},{3,1},{4,6},{6,4},{5,7},{7,5},{8,10},{10,8},{9,1... | collective-permute-start | bytes 3145736 | tf_op jit(solution)/shard_map/ppermute | solution.py:1102
  124.0 57.9 %collective-permute-start.27 = (bf16[512,1024]{1,0:T(8,128)(2,1)}, bf16[512,1024]{1,0:T(8,128)(2,1)}, u32[]{:S(2)}, u32[]{:S(2)}) collective-permute-start(bf16[512,1024]{1,0:T(8,128)(2,1)} %collective-permute-done.10.refs_8_), channel_id=1, source_target_pairs={{0,2},{2,0},{1,3},{3,1},{4,6},{6,4},{5,7},{7,5},{8,10},{10,8},{9,1... | collective-permute-start | bytes 3145736 | tf_op jit(solution)/shard_map/ppermute | solution.py:1102
  127.0 54.9 %collective-permute-start.28 = (bf16[512,1024]{1,0:T(8,128)(2,1)}, bf16[512,1024]{1,0:T(8,128)(2,1)}, u32[]{:S(2)}, u32[]{:S(2)}) collective-permute-start(bf16[512,1024]{1,0:T(8,128)(2,1)} %collective-permute-done.11.refs_9_), channel_id=1, source_target_pairs={{0,2},{2,0},{1,3},{3,1},{4,6},{6,4},{5,7},{7,5},{8,10},{10,8},{9,1... | collective-permute-start | bytes 3145736 | tf_op jit(solution)/shard_map/ppermute | solution.py:1102
  178.1 44.0 %all-to-all-start.1 = ((bf16[8,512,128]{2,1,0:T(8,128)(2,1)}), bf16[8,512,128]{2,1,0:T(8,128)(2,1)S(1)}, u32[]{:S(2)}, u32[]{:S(2)}) async-start(bf16[8,512,128]{2,1,0:T(8,128)(2,1)} %get-tuple-element.149.mixed_ref), calls=%async_computation.1 | async-start | bytes 2097152 | tf_op jit(solution)/shard_map/all_to_all | solution.py:1110
  222.1 18.8 %all-to-all-start.2 = ((bf16[8,512,128]{2,1,0:T(8,128)(2,1)}), bf16[8,512,128]{2,1,0:T(8,128)(2,1)S(1)}, u32[]{:S(2)}, u32[]{:S(2)}) async-start(bf16[8,512,128]{2,1,0:T(8,128)(2,1)} %get-tuple-element.146.mixed_ref), calls=%async_computation.2 | async-start | bytes 2097152 | tf_op jit(solution)/shard_map/all_to_all | solution.py:1110
  226.4 102.6 %all-gather.5.cloned.1.call-start = ((), (), s32[]{:S(2)}) async-start(), calls=%async_computation.12 | async-start | bytes 6488064 | tf_op jit(solution)/shard_map/all_gather | solution.py:1208
  329.0 15.0 %collective-permute-start.29 = (bf16[2,2,4,64,4608]{4,3,2,1,0:T(8,128)(2,1)}, bf16[2,2,4,64,4608]{4,3,2,1,0:T(8,128)(2,1)}, u32[]{:S(2)}, u32[]{:S(2)}) collective-permute-start(bf16[2,2,4,64,4608]{4,3,2,1,0:T(8,128)(2,1)} %get-tuple-element.144), channel_id=1, source_target_pairs={{0,2},{2,0},{1,3},{3,1},{4,6},{6,4},{5,7},{7,5},{8,10},{10,8},{9,1... | collective-permute-start | bytes 28311560 | tf_op jit(solution)/shard_map/ppermute | solution.py:1102
  333.0 21.3 %all-to-all-start.4 = ((bf16[8,512,128]{2,1,0:T(8,128)(2,1)}), bf16[8,512,128]{2,1,0:T(8,128)(2,1)S(1)}, u32[]{:S(2)}, u32[]{:S(2)}) async-start(bf16[8,512,128]{2,1,0:T(8,128)(2,1)} %grad_mixed.3), calls=%async_computation.4 | async-start | bytes 2097152 | tf_op jit(solution)/shard_map/all_to_all | solution.py:1110
  336.6 177.0 %reduce-scatter.3.cloned.1.call-start = ((), (), s32[]{:S(2)}) async-start(), calls=%async_computation.13 | async-start | bytes 11796480 | tf_op jit(solution)/shard_map/reduce_scatter | solution.py:1222
  359.3 42.2 %all-to-all-start.3 = ((bf16[8,512,128]{2,1,0:T(8,128)(2,1)}), bf16[8,512,128]{2,1,0:T(8,128)(2,1)S(1)}, u32[]{:S(2)}, u32[]{:S(2)}) async-start(bf16[8,512,128]{2,1,0:T(8,128)(2,1)} %grad_mixed.2), calls=%async_computation.3 | async-start | bytes 2097152 | tf_op jit(solution)/shard_map/all_to_all | solution.py:1110
  402.6 93.7 %all-to-all-start.6 = ((bf16[8,512,384]{2,1,0:T(8,128)(2,1)}), bf16[8,512,384]{2,1,0:T(8,128)(2,1)S(1)}, u32[]{:S(2)}, u32[]{:S(2)}) async-start(bf16[8,512,384]{2,1,0:T(8,128)(2,1)} %attend_back.2.gq_ref), calls=%async_computation.6 | async-start | bytes 6291456 | tf_op jit(solution)/shard_map/all_to_all | solution.py:1110
  491.9 20.0 %collective-permute-start.30 = (bf16[256,384]{1,0:T(8,128)(2,1)}, bf16[256,384]{1,0:T(8,128)(2,1)S(1)}, u32[]{:S(2)}, u32[]{:S(2)}) collective-permute-start(bf16[256,384]{1,0:T(8,128)(2,1)} %get-tuple-element.166), channel_id=1, source_target_pairs={{0,8},{8,0},{16,24},{24,16},{1,9},{9,1},{17,25},{25,17},{2,10},{10... | collective-permute-start | bytes 589832 | tf_op jit(solution)/shard_map/ppermute | solution.py:1102
  491.9 20.0 %collective-permute-start.31 = (bf16[256,384]{1,0:T(8,128)(2,1)}, bf16[256,384]{1,0:T(8,128)(2,1)S(1)}, u32[]{:S(2)}, u32[]{:S(2)}) collective-permute-start(bf16[256,384]{1,0:T(8,128)(2,1)} %get-tuple-element.167), channel_id=1, source_target_pairs={{0,16},{8,24},{16,0},{24,8},{1,17},{9,25},{17,1},{25,9},{2,18},{10... | collective-permute-start | bytes 589832 | tf_op jit(solution)/shard_map/ppermute | solution.py:1102
  491.9 20.0 %collective-permute-start.32 = (bf16[256,384]{1,0:T(8,128)(2,1)}, bf16[256,384]{1,0:T(8,128)(2,1)}, u32[]{:S(2)}, u32[]{:S(2)}) collective-permute-start(bf16[256,384]{1,0:T(8,128)(2,1)} %get-tuple-element.168), channel_id=1, source_target_pairs={{0,24},{8,16},{16,8},{24,0},{1,25},{9,17},{17,9},{25,1},{2,26},{10... | collective-permute-start | bytes 589832 | tf_op jit(solution)/shard_map/ppermute | solution.py:1102
  497.9 41.7 %all-to-all-start.5 = ((bf16[8,512,384]{2,1,0:T(8,128)(2,1)}), bf16[8,512,384]{2,1,0:T(8,128)(2,1)}, u32[]{:S(2)}, u32[]{:S(2)}) async-start(bf16[8,512,384]{2,1,0:T(8,128)(2,1)} %attend_back.3.gq_ref), calls=%async_computation.5 | async-start | bytes 6291456 | tf_op jit(solution)/shard_map/all_to_all | solution.py:1110
  502.6 75.9 %reduce-scatter.5.cloned.1.call-start = ((), (), s32[]{:S(2)}) async-start(), calls=%async_computation.14 | async-start | bytes 2949120 | tf_op jit(solution)/shard_map/reduce_scatter | solution.py:1246
  502.6 9.2 %copy-start.11 = (bf16[256,384]{1,0:T(8,128)(2,1)S(1)}, bf16[256,384]{1,0:T(8,128)(2,1)}, u32[]{:S(2)}) copy-start(bf16[256,384]{1,0:T(8,128)(2,1)} %get-tuple-element.165) | copy-start | bytes 589828
  513.6 35.9 %copy-start.15 = (f32[1,1024]{1,0:T(1,128)S(1)}, f32[1,1024]{1,0:T(1,128)}, u32[]{:S(2)}) copy-start(f32[1,1024]{1,0:T(1,128)} %get-tuple-element.169) | copy-start | bytes 12292
  513.7 39.3 %copy-start.17 = (f32[2,16]{1,0:T(2,128)S(1)}, f32[2,16]{1,0:T(2,128)}, u32[]{:S(2)}) copy-start(f32[2,16]{1,0:T(2,128)} %copy-done.16) | copy-start | bytes 388
  513.7 39.3 %copy-start.19 = (f32[2,16]{1,0:T(2,128)S(1)}, f32[2,16]{1,0:T(2,128)}, u32[]{:S(2)}) copy-start(f32[2,16]{1,0:T(2,128)} %copy-done.18) | copy-start | bytes 388
  513.7 39.3 %copy-start.21 = (f32[2,16]{1,0:T(2,128)S(1)}, f32[2,16]{1,0:T(2,128)}, u32[]{:S(2)}) copy-start(f32[2,16]{1,0:T(2,128)} %copy-done.20) | copy-start | bytes 388
  513.7 39.3 %copy-start.23 = (f32[2,16]{1,0:T(2,128)S(1)}, f32[2,16]{1,0:T(2,128)}, u32[]{:S(2)}) copy-start(f32[2,16]{1,0:T(2,128)} %copy-done.22) | copy-start | bytes 388
  513.7 39.3 %copy-start.6 = (bf16[512,1024]{1,0:T(8,128)(2,1)S(1)}, bf16[512,1024]{1,0:T(8,128)(2,1)}, u32[]{:S(2)}) copy-start(bf16[512,1024]{1,0:T(8,128)(2,1)} %get-tuple-element.160) | copy-start | bytes 3145732
  550.3 17.5 %all-to-all-start.7 = ((bf16[32,4,1024]{2,1,0:T(4,128)(2,1)}), bf16[32,4,1024]{2,1,0:T(4,128)(2,1)S(1)}, u32[]{:S(2)}, u32[]{:S(2)}) async-start(bf16[32,4,1024]{2,1,0:T(4,128)(2,1)} %broadcast_in_dim.26), calls=%async_computation.8 | async-start | bytes 524288 | tf_op jit(solution)/shard_map/all_to_all | solution.py:1110
  567.8 8.7 %all-to-all-start.8 = ((bf16[4,64,384]{2,1,0:T(8,128)(2,1)}), bf16[4,64,384]{2,1,0:T(8,128)(2,1)S(1)}, u32[]{:S(2)}, u32[]{:S(2)}) async-start(bf16[4,64,384]{2,1,0:T(8,128)(2,1)} %bitcast.26), calls=%async_computation.9 | async-start | bytes 393216 | tf_op jit(solution)/shard_map/all_to_all | solution.py:1110
  (10 other events, 18.9 us)
Sparse Core Ops, SparseCore 0:
  39.6 147.7 all-gather.2
  246.9 72.9 all-gather.4
  354.5 140.0 reduce-scatter.2
  513.7 50.4 reduce-scatter.4
where the time goes:
time: 599 us; the launch traced here: 589 us
  Pallas kernels  330 us (55%)
  waiting for transfers between devices  134 us (22%)
  starting transfers between devices  64.2 us (11%)
  other arithmetic  25.5 us (4%)
  local copies, waits for them, and re-layouts  18.2 us (3%)
  between operations  14.6 us (2%)
    pallas_call x2, Pallas kernels, attend_back(): pl.pallas_call(functools.partial(attend_back_kernel, row=row), grid_spec=...  101 us
    ppermute x33, waiting for transfers between devices, across(): return lax.ppermute(values, axis, [(i, i ^ apart) for i in range(size)])  81 us
    pallas_call x1, Pallas kernels, mlp(): pl.pallas_call(mlp_kernel, grid_spec=pltpu.PrefetchScalarGridSpec(num_sca...  74.9 us
    pallas_call x2, Pallas kernels, attend(): pl.pallas_call(functools.partial(attend_kernel, row=row), grid_spec=pltpu...  61.5 us
    all_to_all x9, waiting for transfers between devices, exchange(): return lax.all_to_all(values, axes, 0, 0, tiled=True)  52.8 us
    all_to_all x9, starting transfers between devices, exchange(): return lax.all_to_all(values, axes, 0, 0, tiled=True)  33.2 us
    ppermute x33, starting transfers between devices, across(): return lax.ppermute(values, axis, [(i, i ^ apart) for i in range(size)])  30.9 us
    pallas_call x2, Pallas kernels, project(): pl.pallas_call(functools.partial(project_kernel, row=row, pieces=pieces,...  26.5 us
  transfers between devices with their start and end apart: 46, of which 15 were waited for; matrix products, arithmetic and copies ran while one was open for 6% of the time, Pallas kernels for 55%

commit v1 on v0

--- a/solution.py
+++ b/solution.py
@@ -349,7 +349,7 @@
 
 
 def transposed(values):
-    return values.astype(jnp.float32).T.astype(values.dtype)
+    return values.T
 
 
 def turned_apart(into_ref, values, core, chunks):

time: 599 us -> 603 us (level); the launches traced: 589 us -> 602 us
  Pallas kernels: 330 us -> 344 us
    pallas_call x2, Pallas kernels: 101 us -> 111 us  [attend_back(): pl.pallas_call(functools.partial(attend_back_kernel, row=row), grid_spec=...]
  transfers between devices with their start and end apart: 46 -> 46, of which waited for: 15 -> 15; matrix products, arithmetic and copies ran while one was open for 6% -> 6% of each run, Pallas kernels for 55% -> 56%
where the time goes in v1:
time: 603 us; the launch traced here: 602 us
  Pallas kernels  344 us (57%)
  waiting for transfers between devices  134 us (22%)
  starting transfers between devices  64 us (11%)
  other arithmetic  25.5 us (4%)
  local copies, waits for them, and re-layouts  18.2 us (3%)
  between operations  14.6 us (2%)
    pallas_call x2, Pallas kernels, attend_back(): pl.pallas_call(functools.partial(attend_back_kernel, row=row), grid_spec=...  111 us
    ppermute x33, waiting for transfers between devices, across(): return lax.ppermute(values, axis, [(i, i ^ apart) for i in range(size)])  81.1 us
    pallas_call x1, Pallas kernels, mlp(): pl.pallas_call(mlp_kernel, grid_spec=pltpu.PrefetchScalarGridSpec(num_sca...  74.8 us
    pallas_call x2, Pallas kernels, attend(): pl.pallas_call(functools.partial(attend_kernel, row=row), grid_spec=pltpu...  66 us
    all_to_all x9, waiting for transfers between devices, exchange(): return lax.all_to_all(values, axes, 0, 0, tiled=True)  52.6 us
    all_to_all x9, starting transfers between devices, exchange(): return lax.all_to_all(values, axes, 0, 0, tiled=True)  33 us
    ppermute x33, starting transfers between devices, across(): return lax.ppermute(values, axis, [(i, i ^ apart) for i in range(size)])  30.9 us
    pallas_call x2, Pallas kernels, project(): pl.pallas_call(functools.partial(project_kernel, row=row, pieces=pieces,...  26.5 us
  transfers between devices with their start and end apart: 46, of which 15 were waited for; matrix products, arithmetic and copies ran while one was open for 6% of the time, Pallas kernels for 56%

profile of v1, /device:TPU:0, one launch (start us, length us, event | category | flops | bytes accessed | tf_op | source)
XLA Modules:
  0.0 601.6 jit_solution(12715186628243134625)
XLA Ops:
  7.2 1.8 slice_bitcast_fusion
  9.0 3.0 collective-permute-start
  12.0 1.5 collective-permute-start.1
  13.6 1.6 collective-permute-start.2
  15.1 2.6 collective-permute-start.3
  18.7 3.4 all-to-all-start
  22.1 1.5 convert_element_type.62
  25.2 1.7 collective-permute-start.6
  27.8 11.6 %collective-permute-done.6 = bf16[16,2048]{1,0:T(8,128)(2,1)S(1)} collective-permute-done((bf16[16,2048]{1,0:T(8,128)(2,1)}, bf16[16,2048]{1,0:T(8,128)(2,1)S(1)}, u32[]{:S(2)}, u32[]{:S(2)}) %collective-permute-start.6) | collective-permute-done | bytes 65568 | tf_op jit(solution)/shard_map/ppermute | solution.py:1102
  41.7 1.7 collective-permute-start.19
  46.6 1.1 fusion
  47.7 1.6 collective-permute-start.12
  49.4 2.6 collective-permute-start.13
  53.1 1.4 collective-permute-start.10
  55.1 1.5 collective-permute-start.8
  57.4 1.3 collective-permute-done.14
  59.4 11.5 %collective-permute-done.15.refs_1_ = bf16[256,384]{1,0:T(8,128)(2,1)S(1)} collective-permute-done((bf16[256,384]{1,0:T(8,128)(2,1)S(1)}, bf16[256,384]{1,0:T(8,128)(2,1)S(1)}, u32[]{:S(2)}, u32[]{:S(2)}) %collective-permute-start.15) | collective-permute-done | bytes 196640 | tf_op jit(solution)/shard_map/ppermute | solution.py:1102
  72.1 20.4 %collective-permute-done.16.refs_2_ = bf16[256,384]{1,0:T(8,128)(2,1)S(1)} collective-permute-done((bf16[256,384]{1,0:T(8,128)(2,1)S(1)}, bf16[256,384]{1,0:T(8,128)(2,1)S(1)}, u32[]{:S(2)}, u32[]{:S(2)}) %collective-permute-start.16) | collective-permute-done | bytes 196640 | tf_op jit(solution)/shard_map/ppermute | solution.py:1102
  92.6 2.2 collective-permute-start.17
  95.4 5.7 collective-permute-done.17.refs_3_
  101.1 17.6 %collective-permute-done.11.refs_9_ = bf16[512,1024]{1,0:T(8,128)(2,1)} collective-permute-done((bf16[512,1024]{1,0:T(8,128)(2,1)}, bf16[512,1024]{1,0:T(8,128)(2,1)}, u32[]{:S(2)}, u32[]{:S(2)}) %collective-permute-start.11) | collective-permute-done | bytes 1048608 | tf_op jit(solution)/shard_map/ppermute | solution.py:1102
  120.4 2.7 copy.83.segc_ref
  124.1 2.9 collective-permute-done.23.refs_10_
  127.1 2.1 collective-permute-done.24.refs_11_
  129.2 13.3 %project.2 = (bf16[8,512,384]{2,1,0:T(8,128)(2,1)}, bf16[8,512,1024]{2,1,0:T(8,128)(2,1)}) custom-call(s32[3]{0:T(128)} %pad_add_fusion.3.place_ref, f32[2,2048]{1,0:T(2,128)} %fusion.9.scales_ref, bf16[256,384]{1,0:T(8,128)(2,1)} %bitcast.77, bf16[256,384]{1,0:T(8,128)(2,1)} %copy-done.25, bf16[256,384]{1,0:T(8,128)(2,1)} %copy-done.26, ...), custom_call_target="tpu_custom_call" | custom-call | flops 3221225472 | bytes 20971520 | tf_op jit(solution)/shard_map/project/pallas_call | solution.py:425
  142.5 35.5 %attend.2 = (bf16[8,512,128]{2,1,0:T(8,128)(2,1)}, f32[2,4096]{1,0:T(2,128)}) custom-call(s32[2,64]{1,0:T(2,128)} %convert_element_type.63.listed_ref, s32[2,32]{1,0:T(2,128)} %pad_add_fusion.2.edge_ref, bf16[8,512,384]{2,1,0:T(8,128)(2,1)} %get-tuple-element.115.qkv_ref, s32[2,4096,1]{2,1,0:T(8,128)} %copy.83.segc_ref, s32[2,1,4096]{2,1,0:T(1,128)} %broadcast_in_dim.25.segr_ref), custom_call_target="tpu_custom_call" | custom-call | flops 20000000000 | bytes 6000000 | tf_op jit(solution)/shard_map/attend/pallas_call | solution.py:609
  178.0 3.8 all-to-all-start.1
  182.8 13.2 %project.3 = (bf16[8,512,384]{2,1,0:T(8,128)(2,1)}, bf16[8,512,1024]{2,1,0:T(8,128)(2,1)}) custom-call(s32[3]{0:T(128)} %pad_add_fusion.3.place_ref, f32[2,2048]{1,0:T(2,128)} %fusion.9.scales_ref, bf16[256,384]{1,0:T(8,128)(2,1)} %bitcast.78, bf16[256,384]{1,0:T(8,128)(2,1)} %copy-done.25, bf16[256,384]{1,0:T(8,128)(2,1)} %copy-done.26, ...), custom_call_target="tpu_custom_call" | custom-call | flops 3221225472 | bytes 20971520 | tf_op jit(solution)/shard_map/project/pallas_call | solution.py:425
  196.0 30.5 %attend.3 = (bf16[8,512,128]{2,1,0:T(8,128)(2,1)}, f32[2,4096]{1,0:T(2,128)}) custom-call(s32[2,64]{1,0:T(2,128)} %convert_element_type.63.listed_ref, s32[2,32]{1,0:T(2,128)} %pad_add_fusion.2.edge_ref, bf16[8,512,384]{2,1,0:T(8,128)(2,1)} %get-tuple-element.123.qkv_ref, s32[2,4096,1]{2,1,0:T(8,128)} %copy.83.segc_ref, s32[2,1,4096]{2,1,0:T(1,128)} %broadcast_in_dim.25.segr_ref), custom_call_target="tpu_custom_call" | custom-call | flops 20000000000 | bytes 6000000 | tf_op jit(solution)/shard_map/attend/pallas_call | solution.py:609
  226.5 4.3 all-to-all-start.2
  230.9 4.9 outward.2
  235.8 9.6 %all-to-all-done.2.mixed_ref.mixed1_ref = bf16[8,512,128]{2,1,0:T(8,128)(2,1)S(1)} async-done(((bf16[8,512,128]{2,1,0:T(8,128)(2,1)}), bf16[8,512,128]{2,1,0:T(8,128)(2,1)S(1)}, u32[]{:S(2)}, u32[]{:S(2)}) %all-to-all-start.2) | async-done | bytes 1048608 | tf_op jit(solution)/shard_map/all_to_all | solution.py:1110
  245.4 1.0 copy-done.2
  246.4 4.8 outward.3
  251.2 74.8 %mlp.1 = (bf16[2,2,4,64,4608]{4,3,2,1,0:T(8,128)(2,1)}, bf16[2,2,4,64,4608]{4,3,2,1,0:T(8,128)(2,1)}, bf16[1024,1024]{1,0:T(8,128)(2,1)}, f32[1024,1024]{1,0:T(8...) custom-call(s32[3]{0:T(128)} %pad_add_fusion.3.place_ref, bf16[512,1024]{1,0:T(8,128)(2,1)} %get-tuple-element.131.nm0_ref, ...), custom_call_target="tpu_custom_call" | custom-call | flops 51539607552 | bytes 54525952 | tf_op jit(solution)/shard_map/mlp/pallas_call | solution.py:870
  326.0 7.3 %grad_proj.1 = (bf16[2,2,4,64,4608]{4,3,2,1,0:T(8,128)(2,1)}, bf16[2,2,4,64,4608]{4,3,2,1,0:T(8,128)(2,1)}) custom-call(s32[3]{0:T(128)} %pad_add_fusion.3.place_ref, bf16[1024,1024]{1,0:T(8,128)(2,1)} %get-tuple-element.142.grad_ref, bf16[8,512,128]{2,1,0:T(8,128)(2,1)} %copy-done.1, ...), custom_call_target="tpu_custom_call", output_to_operand_aliasing={{0}: (4, {}), {1}: (5, {})} | custom-call | flops 2147483648 | bytes 6291456 | tf_op jit(solution)/shard_map/grad_proj/pallas_call | solution.py:970
  333.3 4.0 grad_mixed.3
  337.3 3.6 all-to-all-start.4
  340.9 7.4 %collective-permute-done.29 = bf16[2,2,4,64,4608]{4,3,2,1,0:T(8,128)(2,1)} collective-permute-done((bf16[2,2,4,64,4608]{4,3,2,1,0:T(8,128)(2,1)}, bf16[2,2,4,64,4608]{4,3,2,1,0:T(8,128)(2,1)}, u32[]{:S(2)}, u32[]{:S(2)}) %collective-permute-start.29) | collective-permute-done | bytes 9437216 | tf_op jit(solution)/shard_map/ppermute | solution.py:1102
  348.3 10.3 %add_convert_fusion = bf16[2,2,4,64,4608]{4,3,2,1,0:T(8,128)(2,1)} fusion(bf16[2,2,4,64,4608]{4,3,2,1,0:T(8,128)(2,1)} %collective-permute-done.29, bf16[2,2,4,64,4608]{4,3,2,1,0:T(8,128)(2,1)} %get-tuple-element.143), kind=kLoop, calls=%fused_computation | loop fusion | flops 18874368 | bytes 28311552 | tf_op jit(solution)/shard_map/convert_element_type | solution.py:1220
  358.7 0.9 copy-done.4
  359.6 4.0 grad_mixed.2
  363.6 3.6 all-to-all-start.3
  367.2 48.2 %attend_back.2.gq_ref = bf16[8,512,384]{2,1,0:T(8,128)(2,1)} custom-call(s32[2,64]{1,0:T(2,128)} %convert_element_type.63.listed_ref, s32[2,32]{1,0:T(2,128)} %pad_add_fusion.2.edge_ref, bf16[8,512,384]{2,1,0:T(8,128)(2,1)} %get-tuple-element.123.qkv_ref, bf16[8,512,128]{2,1,0:T(8,128)(2,1)} %copy-done.4, bf16[8,512,128]{2,1,0:T(8,128)(2,1)} %get-tuple-element.146.mixed_ref, ...), custom_call_target="tpu_custom_call" | custom-call | flops 49999998976 | bytes 10000000 | tf_op jit(solution)/shard_map/attend_back/pallas_call | solution.py:718
  415.4 1.0 copy-done.5
  416.4 3.9 all-to-all-start.6
  420.3 62.5 %attend_back.3.gq_ref = bf16[8,512,384]{2,1,0:T(8,128)(2,1)} custom-call(s32[2,64]{1,0:T(2,128)} %convert_element_type.63.listed_ref, s32[2,32]{1,0:T(2,128)} %pad_add_fusion.2.edge_ref, bf16[8,512,384]{2,1,0:T(8,128)(2,1)} %get-tuple-element.115.qkv_ref, bf16[8,512,128]{2,1,0:T(8,128)(2,1)} %copy-done.5, bf16[8,512,128]{2,1,0:T(8,128)(2,1)} %get-tuple-element.149.mixed_ref, ...), custom_call_target="tpu_custom_call" | custom-call | flops 49999998976 | bytes 10000000 | tf_op jit(solution)/shard_map/attend_back/pallas_call | solution.py:718
  482.8 10.7 %grad_qkv.2.refs_0_ = f32[384,1024]{1,0:T(8,128)} custom-call(s32[3]{0:T(128)} %pad_add_fusion.3.place_ref, bf16[8,512,1024]{2,1,0:T(8,128)(2,1)} %get-tuple-element.156.normed_ref, bf16[8,512,384]{2,1,0:T(8,128)(2,1)} %attend_back.2.gq_ref), custom_call_target="tpu_custom_call" | custom-call | flops 3221225472 | bytes 12582912 | tf_op jit(solution)/shard_map/grad_qkv/pallas_call | solution.py:1069
  493.4 11.4 %grad_qkv.3 = (bf16[256,384]{1,0:T(8,128)(2,1)}, bf16[256,384]{1,0:T(8,128)(2,1)}, bf16[256,384]{1,0:T(8,128)(2,1)}, bf16[256,384]{1,0:T(8,128)(2,1)}) custom-call(s32[3]{0:T(128)} %pad_add_fusion.3.place_ref, bf16[8,512,1024]{2,1,0:T(8,128)(2,1)} %get-tuple-element.155.normed_ref, bf16[8,512,384]{2,1,0:T(8,128)(2,1)} %attend_back.3.gq_ref, ...), custom_call_target="tpu_custom_call" | custom-call | flops 3221225472 | bytes 12582912 | tf_op jit(solution)/shard_map/grad_qkv/pallas_call | solution.py:1069
  504.9 4.3 collective-permute-start.32
  509.2 1.7 copy-done
  510.9 4.7 all-to-all-start.5
  515.6 9.2 %first_norm_back.3 = (bf16[512,1024]{1,0:T(8,128)(2,1)}, f32[1,1024]{1,0:T(1,128)}) custom-call(bf16[8,512,384]{2,1,0:T(8,128)(2,1)} %copy-done, bf16[2,512,1024]{2,1,0:T(8,128)(2,1)} %tok_ref.7, f32[1024,1024]{1,0:T(8,128)} %get-tuple-element.151.grad_hidden_ref, bf16[16,2,64,1536]{3,2,1,0:T(8,128)(2,1)} %bitcast.68, f32[2,2048]{1,0:T(2,128)} %fusion.9.scales_ref), custom_call_target="tpu_custom_call" | custom-call | flops 3221225472 | bytes 16777216 | tf_op jit(solution)/shard_map/first_norm_back/pallas_call | solution.py:1016
  524.8 1.7 add_convert_fusion.1
  526.7 25.9 %all-to-all-done.5.gq_ref = bf16[8,512,384]{2,1,0:T(8,128)(2,1)} async-done(((bf16[8,512,384]{2,1,0:T(8,128)(2,1)}), bf16[8,512,384]{2,1,0:T(8,128)(2,1)}, u32[]{:S(2)}, u32[]{:S(2)}) %all-to-all-start.5) | async-done | bytes 3145760 | tf_op jit(solution)/shard_map/all_to_all | solution.py:1110
  552.6 9.2 %first_norm_back.2 = (bf16[512,1024]{1,0:T(8,128)(2,1)}, f32[1,1024]{1,0:T(1,128)}) custom-call(bf16[8,512,384]{2,1,0:T(8,128)(2,1)} %all-to-all-done.5.gq_ref, bf16[2,512,1024]{2,1,0:T(8,128)(2,1)} %tok_ref.7, f32[1024,1024]{1,0:T(8,128)} %get-tuple-element.151.grad_hidden_ref, bf16[16,2,64,1536]{3,2,1,0:T(8,128)(2,1)} %bitcast.69, f32[2,2048]{1,0:T(2,128)} %fusion.9.scales_ref), custom_call_target="tpu_custom_call" | custom-call | flops 3221225472 | bytes 16777216 | tf_op jit(solution)/shard_map/first_norm_back/pallas_call | solution.py:1016
  563.3 2.6 all-to-all-start.7
  566.0 2.7 pad_maximum_fusion
  568.7 11.9 %all-to-all-done.7 = bf16[32,4,1024]{2,1,0:T(4,128)(2,1)S(1)} async-done(((bf16[32,4,1024]{2,1,0:T(4,128)(2,1)}), bf16[32,4,1024]{2,1,0:T(4,128)(2,1)S(1)}, u32[]{:S(2)}, u32[]{:S(2)}) %all-to-all-start.7) | async-done | bytes 262176 | tf_op jit(solution)/shard_map/all_to_all | solution.py:1110
  580.6 3.4 all-to-all-start.8
  584.0 5.2 all-to-all-done.8
  590.3 1.0 fusion.41
  591.2 2.1 slice_convert_fusion
  593.4 1.5 slice_convert_fusion.2
  (166 shorter events, 20.5 us)
Async XLA Ops:
  7.2 6.4 %copy-start.14 = (f32[2,256]{1,0:T(2,128)S(1)}, f32[2,256]{1,0:T(2,128)}, u32[]{:S(2)}) copy-start(f32[2,256]{1,0:T(2,128)} %param.12) | copy-start | bytes 6148
  7.2 10.8 %copy-start.9 = (f32[64,1536]{1,0:T(8,128)S(1)}, f32[64,1536]{1,0:T(8,128)}, u32[]{:S(2)}) copy-start(f32[64,1536]{1,0:T(8,128)} %param.17) | copy-start | bytes 1179652
  7.2 16.5 %copy-start.7 = (f32[64,2048]{1,0:T(8,128)S(1)}, f32[64,2048]{1,0:T(8,128)}, u32[]{:S(2)}) copy-start(f32[64,2048]{1,0:T(8,128)} %param.19) | copy-start | bytes 1572868
  7.2 16.5 %copy-start.8 = (f32[64,2048]{1,0:T(8,128)S(1)}, f32[64,2048]{1,0:T(8,128)}, u32[]{:S(2)}) copy-start(f32[64,2048]{1,0:T(8,128)} %param.20) | copy-start | bytes 1572868
  9.0 30.5 %collective-permute-start = (bf16[512,1024]{1,0:T(8,128)(2,1)S(1)}, bf16[512,1024]{1,0:T(8,128)(2,1)}, u32[]{:S(2)}, u32[]{:S(2)}) collective-permute-start(bf16[512,1024]{1,0:T(8,128)(2,1)S(1)} %get-tuple-element.112), channel_id=1, source_target_pairs={{0,4},{4,0},{1,5},{5,1},{2,6},{6,2},{3,7},{7,3},{8,12},{12,8},{9,1... | collective-permute-start | bytes 3145736 | tf_op jit(solution)/shard_map/ppermute | solution.py:1102
  12.0 27.4 %collective-permute-start.1 = (bf16[512,1024]{1,0:T(8,128)(2,1)S(1)}, bf16[512,1024]{1,0:T(8,128)(2,1)}, u32[]{:S(2)}, u32[]{:S(2)}) collective-permute-start(bf16[512,1024]{1,0:T(8,128)(2,1)S(1)} %get-tuple-element.120), channel_id=1, source_target_pairs={{0,1},{1,0},{2,3},{3,2},{4,5},{5,4},{6,7},{7,6},{8,9},{9,8},{10,11... | collective-permute-start | bytes 3145736 | tf_op jit(solution)/shard_map/ppermute | solution.py:1102
  13.6 11.1 %collective-permute-start.2 = (f32[2,256]{1,0:T(2,128)S(1)}, f32[2,256]{1,0:T(2,128)S(1)}, u32[]{:S(2)}, u32[]{:S(2)}) collective-permute-start(f32[2,256]{1,0:T(2,128)S(1)} %copy-done.14), channel_id=1, source_target_pairs={{0,8},{8,0},{16,24},{24,16},{1,9},{9,1},{17,25},{25,17},{2,10},{10... | collective-permute-start | bytes 6152 | tf_op jit(solution)/shard_map/ppermute | solution.py:1102
  15.1 10.1 %collective-permute-start.3 = (f32[2,256]{1,0:T(2,128)S(1)}, f32[2,256]{1,0:T(2,128)S(1)}, u32[]{:S(2)}, u32[]{:S(2)}) collective-permute-start(f32[2,256]{1,0:T(2,128)S(1)} %copy-done.14), channel_id=1, source_target_pairs={{0,16},{8,24},{16,0},{24,8},{1,17},{9,25},{17,1},{25,9},{2,18},{10... | collective-permute-start | bytes 6152 | tf_op jit(solution)/shard_map/ppermute | solution.py:1102
  17.7 9.2 %collective-permute-start.4 = (f32[2,256]{1,0:T(2,128)S(1)}, f32[2,256]{1,0:T(2,128)S(1)}, u32[]{:S(2)}, u32[]{:S(2)}) collective-permute-start(f32[2,256]{1,0:T(2,128)S(1)} %copy-done.14), channel_id=1, source_target_pairs={{0,24},{8,16},{16,8},{24,0},{1,25},{9,17},{17,9},{25,1},{2,26},{10... | collective-permute-start | bytes 6152 | tf_op jit(solution)/shard_map/ppermute | solution.py:1102
  18.0 105.1 %copy-start.3 = (bf16[64,1536]{1,0:T(8,128)(2,1)}, bf16[64,1536]{1,0:T(8,128)(2,1)S(1)}, u32[]{:S(2)}) copy-start(bf16[64,1536]{1,0:T(8,128)(2,1)S(1)} %convert_element_type.61) | copy-start | bytes 589828
  18.7 20.8 %all-to-all-start = ((bf16[4,64,384]{2,1,0:T(8,128)(2,1)}), bf16[4,64,384]{2,1,0:T(8,128)(2,1)S(1)}, u32[]{:S(2)}, u32[]{:S(2)}) async-start(bf16[4,64,384]{2,1,0:T(8,128)(2,1)} %bitcast.59), calls=%async_computation | async-start | bytes 393216 | tf_op jit(solution)/shard_map/all_to_all | solution.py:1110
  22.1 208.8 %all-gather.3.cloned.1.call-start = ((), (), s32[]{:S(2)}) async-start(), calls=%async_computation.11 | async-start | bytes 19464192 | tf_op jit(solution)/shard_map/all_gather | solution.py:1168
  23.7 28.3 %copy-start.12 = (s32[2,4096]{1,0:T(2,128)S(1)}, s32[2,4096]{1,0:T(2,128)}, u32[]{:S(2)}) copy-start(s32[2,4096]{1,0:T(2,128)} %param.13) | copy-start | bytes 98308
  24.7 3.1 collective-permute-start.5
  25.2 14.2 %collective-permute-start.6 = (bf16[16,2048]{1,0:T(8,128)(2,1)}, bf16[16,2048]{1,0:T(8,128)(2,1)S(1)}, u32[]{:S(2)}, u32[]{:S(2)}) collective-permute-start(bf16[16,2048]{1,0:T(8,128)(2,1)} %convert_element_type.62), channel_id=1, source_target_pairs={{0,4},{2,6},{4,0},{6,2},{1,5},{3,7},{5,1},{7,3},{8,12},{10,14},{12... | collective-permute-start | bytes 196616 | tf_op jit(solution)/shard_map/ppermute | solution.py:1102
  26.9 12.6 %collective-permute-start.7 = (bf16[16,2048]{1,0:T(8,128)(2,1)}, bf16[16,2048]{1,0:T(8,128)(2,1)S(1)}, u32[]{:S(2)}, u32[]{:S(2)}) collective-permute-start(bf16[16,2048]{1,0:T(8,128)(2,1)} %convert_element_type.62), channel_id=1, source_target_pairs={{0,6},{2,4},{4,2},{6,0},{1,7},{3,5},{5,3},{7,1},{8,14},{10,12},{12... | collective-permute-start | bytes 196616 | tf_op jit(solution)/shard_map/ppermute | solution.py:1102
  39.5 83.6 %copy-start.10 = (bf16[4,64,384]{2,1,0:T(8,128)(2,1)}, bf16[4,64,384]{2,1,0:T(8,128)(2,1)S(1)}, u32[]{:S(2)}) copy-start(bf16[4,64,384]{2,1,0:T(8,128)(2,1)S(1)} %all-to-all-done) | copy-start | bytes 589828
  41.2 11.6 %collective-permute-start.18 = (s32[2,1,31]{2,0,1:T(2,128)S(1)}, s32[2,1,31]{2,0,1:T(2,128)S(1)}, u32[]{:S(2)}, u32[]{:S(2)}) collective-permute-start(s32[2,1,31]{2,0,1:T(2,128)S(1)} %pad_add_fusion.1), channel_id=1, source_target_pairs={{0,2},{2,0},{4,6},{6,4},{1,3},{3,1},{5,7},{7,5},{8,10},{10,8},{12,... | collective-permute-start | bytes 752 | tf_op jit(solution)/shard_map/ppermute | solution.py:1102
  41.7 11.4 %collective-permute-start.19 = (s32[2,1,31]{2,0,1:T(2,128)S(1)}, s32[2,1,31]{2,0,1:T(2,128)S(1)}, u32[]{:S(2)}, u32[]{:S(2)}) collective-permute-start(s32[2,1,31]{2,0,1:T(2,128)S(1)} %pad_add_fusion.1), channel_id=1, source_target_pairs={{0,4},{2,6},{4,0},{6,2},{1,5},{3,7},{5,1},{7,3},{8,12},{10,14},{12... | collective-permute-start | bytes 752 | tf_op jit(solution)/shard_map/ppermute | solution.py:1102
  43.5 11.1 %collective-permute-start.20 = (s32[2,1,31]{2,0,1:T(2,128)S(1)}, s32[2,1,31]{2,0,1:T(2,128)S(1)}, u32[]{:S(2)}, u32[]{:S(2)}) collective-permute-start(s32[2,1,31]{2,0,1:T(2,128)S(1)} %pad_add_fusion.1), channel_id=1, source_target_pairs={{0,6},{2,4},{4,2},{6,0},{1,7},{3,5},{5,3},{7,1},{8,14},{10,12},{12... | collective-permute-start | bytes 752 | tf_op jit(solution)/shard_map/ppermute | solution.py:1102
  46.0 96.5 %copy-start.20 = (f32[2,16]{1,0:T(2,128)}, f32[2,16]{1,0:T(2,128)S(1)}, u32[]{:S(2)}) copy-start(f32[2,16]{1,0:T(2,128)S(1)} %get-tuple-element.204) | copy-start | bytes 388
  47.7 7.4 %collective-permute-start.12 = (f32[2,2048]{1,0:T(2,128)S(1)}, f32[2,2048]{1,0:T(2,128)S(1)}, u32[]{:S(2)}, u32[]{:S(2)}) collective-permute-start(f32[2,2048]{1,0:T(2,128)S(1)} %get-tuple-element.185), channel_id=1, source_target_pairs={{0,8},{8,0},{16,24},{24,16},{1,9},{9,1},{17,25},{25,17},{2,10},{10... | collective-permute-start | bytes 49160 | tf_op jit(solution)/shard_map/ppermute | solution.py:1102
  49.4 7.3 %collective-permute-start.13 = (f32[2,2048]{1,0:T(2,128)S(1)}, f32[2,2048]{1,0:T(2,128)S(1)}, u32[]{:S(2)}, u32[]{:S(2)}) collective-permute-start(f32[2,2048]{1,0:T(2,128)S(1)} %get-tuple-element.183), channel_id=1, source_target_pairs={{0,16},{8,24},{16,0},{24,8},{1,17},{9,25},{17,1},{25,9},{2,18},{10... | collective-permute-start | bytes 49160 | tf_op jit(solution)/shard_map/ppermute | solution.py:1102
  52.9 5.9 collective-permute-start.14
  53.1 48.0 %collective-permute-start.10 = (bf16[512,1024]{1,0:T(8,128)(2,1)S(1)}, bf16[512,1024]{1,0:T(8,128)(2,1)}, u32[]{:S(2)}, u32[]{:S(2)}) collective-permute-start(bf16[512,1024]{1,0:T(8,128)(2,1)S(1)} %get-tuple-element.120), channel_id=1, source_target_pairs={{0,4},{4,0},{1,5},{5,1},{2,6},{6,2},{3,7},{7,3},{8,12},{12,8},{9,1... | collective-permute-start | bytes 3145736 | tf_op jit(solution)/shard_map/ppermute | solution.py:1102
  54.5 64.2 %collective-permute-start.11 = (bf16[512,1024]{1,0:T(8,128)(2,1)}, bf16[512,1024]{1,0:T(8,128)(2,1)}, u32[]{:S(2)}, u32[]{:S(2)}) collective-permute-start(bf16[512,1024]{1,0:T(8,128)(2,1)} %collective-permute-done.1.refs_5_), channel_id=1, source_target_pairs={{0,4},{4,0},{1,5},{5,1},{2,6},{6,2},{3,7},{7,3},{8,12},{12,8},{9,1... | collective-permute-start | bytes 3145736 | tf_op jit(solution)/shard_map/ppermute | solution.py:1102
  55.1 63.6 %collective-permute-start.8 = (bf16[512,1024]{1,0:T(8,128)(2,1)S(1)}, bf16[512,1024]{1,0:T(8,128)(2,1)}, u32[]{:S(2)}, u32[]{:S(2)}) collective-permute-start(bf16[512,1024]{1,0:T(8,128)(2,1)S(1)} %get-tuple-element.112), channel_id=1, source_target_pairs={{0,1},{1,0},{2,3},{3,2},{4,5},{5,4},{6,7},{7,6},{8,9},{9,8},{10,11... | collective-permute-start | bytes 3145736 | tf_op jit(solution)/shard_map/ppermute | solution.py:1102
  56.7 62.1 %collective-permute-start.9 = (bf16[512,1024]{1,0:T(8,128)(2,1)}, bf16[512,1024]{1,0:T(8,128)(2,1)}, u32[]{:S(2)}, u32[]{:S(2)}) collective-permute-start(bf16[512,1024]{1,0:T(8,128)(2,1)} %collective-permute-done.refs_8_), channel_id=1, source_target_pairs={{0,1},{1,0},{2,3},{3,2},{4,5},{5,4},{6,7},{7,6},{8,9},{9,8},{10,11... | collective-permute-start | bytes 3145736 | tf_op jit(solution)/shard_map/ppermute | solution.py:1102
  58.7 12.1 %collective-permute-start.15 = (bf16[256,384]{1,0:T(8,128)(2,1)S(1)}, bf16[256,384]{1,0:T(8,128)(2,1)S(1)}, u32[]{:S(2)}, u32[]{:S(2)}) collective-permute-start(bf16[256,384]{1,0:T(8,128)(2,1)S(1)} %bitcast.74), channel_id=1, source_target_pairs={{0,8},{8,0},{16,24},{24,16},{1,9},{9,1},{17,25},{25,17},{2,10},{10... | collective-permute-start | bytes 589832 | tf_op jit(solution)/shard_map/ppermute | solution.py:1102
  70.9 58.3 %copy-start.25 = (bf16[256,384]{1,0:T(8,128)(2,1)}, bf16[256,384]{1,0:T(8,128)(2,1)S(1)}, u32[]{:S(2)}) copy-start(bf16[256,384]{1,0:T(8,128)(2,1)S(1)} %collective-permute-done.15.refs_1_) | copy-start | bytes 589828
  70.9 21.7 %collective-permute-start.16 = (bf16[256,384]{1,0:T(8,128)(2,1)S(1)}, bf16[256,384]{1,0:T(8,128)(2,1)S(1)}, u32[]{:S(2)}, u32[]{:S(2)}) collective-permute-start(bf16[256,384]{1,0:T(8,128)(2,1)S(1)} %bitcast.75), channel_id=1, source_target_pairs={{0,16},{8,24},{16,0},{24,8},{1,17},{9,25},{17,1},{25,9},{2,18},{10... | collective-permute-start | bytes 589832 | tf_op jit(solution)/shard_map/ppermute | solution.py:1102
  92.6 30.5 %copy-start.26 = (bf16[256,384]{1,0:T(8,128)(2,1)}, bf16[256,384]{1,0:T(8,128)(2,1)S(1)}, u32[]{:S(2)}) copy-start(bf16[256,384]{1,0:T(8,128)(2,1)S(1)} %collective-permute-done.16.refs_2_) | copy-start | bytes 589828
  92.6 8.5 %collective-permute-start.17 = (bf16[256,384]{1,0:T(8,128)(2,1)S(1)}, bf16[256,384]{1,0:T(8,128)(2,1)S(1)}, u32[]{:S(2)}, u32[]{:S(2)}) collective-permute-start(bf16[256,384]{1,0:T(8,128)(2,1)S(1)} %bitcast.76), channel_id=1, source_target_pairs={{0,24},{8,16},{16,8},{24,0},{1,25},{9,17},{17,9},{25,1},{2,26},{10... | collective-permute-start | bytes 589832 | tf_op jit(solution)/shard_map/ppermute | solution.py:1102
  101.1 22.0 %copy-start.27 = (bf16[256,384]{1,0:T(8,128)(2,1)}, bf16[256,384]{1,0:T(8,128)(2,1)S(1)}, u32[]{:S(2)}) copy-start(bf16[256,384]{1,0:T(8,128)(2,1)S(1)} %collective-permute-done.17.refs_3_) | copy-start | bytes 589828
  118.7 4.4 collective-permute-start.21
  118.7 5.2 collective-permute-start.22
  119.2 7.7 %collective-permute-start.23 = (bf16[512,1024]{1,0:T(8,128)(2,1)}, bf16[512,1024]{1,0:T(8,128)(2,1)}, u32[]{:S(2)}, u32[]{:S(2)}) collective-permute-start(bf16[512,1024]{1,0:T(8,128)(2,1)} %collective-permute-done.refs_8_), channel_id=1, source_target_pairs={{0,2},{2,0},{1,3},{3,1},{4,6},{6,4},{5,7},{7,5},{8,10},{10,8},{9,1... | collective-permute-start | bytes 3145736 | tf_op jit(solution)/shard_map/ppermute | solution.py:1102
  119.3 9.9 %collective-permute-start.24 = (bf16[512,1024]{1,0:T(8,128)(2,1)}, bf16[512,1024]{1,0:T(8,128)(2,1)}, u32[]{:S(2)}, u32[]{:S(2)}) collective-permute-start(bf16[512,1024]{1,0:T(8,128)(2,1)} %collective-permute-done.9.refs_9_), channel_id=1, source_target_pairs={{0,2},{2,0},{1,3},{3,1},{4,6},{6,4},{5,7},{7,5},{8,10},{10,8},{9,1... | collective-permute-start | bytes 3145736 | tf_op jit(solution)/shard_map/ppermute | solution.py:1102
  120.4 61.5 %collective-permute-start.25 = (bf16[512,1024]{1,0:T(8,128)(2,1)S(1)}, bf16[512,1024]{1,0:T(8,128)(2,1)}, u32[]{:S(2)}, u32[]{:S(2)}) collective-permute-start(bf16[512,1024]{1,0:T(8,128)(2,1)S(1)} %get-tuple-element.120), channel_id=1, source_target_pairs={{0,2},{2,0},{1,3},{3,1},{4,6},{6,4},{5,7},{7,5},{8,10},{10,8},{9,1... | collective-permute-start | bytes 3145736 | tf_op jit(solution)/shard_map/ppermute | solution.py:1102
  123.1 58.7 %collective-permute-start.26 = (bf16[512,1024]{1,0:T(8,128)(2,1)}, bf16[512,1024]{1,0:T(8,128)(2,1)S(1)}, u32[]{:S(2)}, u32[]{:S(2)}) collective-permute-start(bf16[512,1024]{1,0:T(8,128)(2,1)} %collective-permute-done.1.refs_5_), channel_id=1, source_target_pairs={{0,2},{2,0},{1,3},{3,1},{4,6},{6,4},{5,7},{7,5},{8,10},{10,8},{9,1... | collective-permute-start | bytes 3145736 | tf_op jit(solution)/shard_map/ppermute | solution.py:1102
  124.0 57.9 %collective-permute-start.27 = (bf16[512,1024]{1,0:T(8,128)(2,1)}, bf16[512,1024]{1,0:T(8,128)(2,1)}, u32[]{:S(2)}, u32[]{:S(2)}) collective-permute-start(bf16[512,1024]{1,0:T(8,128)(2,1)} %collective-permute-done.10.refs_8_), channel_id=1, source_target_pairs={{0,2},{2,0},{1,3},{3,1},{4,6},{6,4},{5,7},{7,5},{8,10},{10,8},{9,1... | collective-permute-start | bytes 3145736 | tf_op jit(solution)/shard_map/ppermute | solution.py:1102
  127.0 54.9 %collective-permute-start.28 = (bf16[512,1024]{1,0:T(8,128)(2,1)}, bf16[512,1024]{1,0:T(8,128)(2,1)}, u32[]{:S(2)}, u32[]{:S(2)}) collective-permute-start(bf16[512,1024]{1,0:T(8,128)(2,1)} %collective-permute-done.11.refs_9_), channel_id=1, source_target_pairs={{0,2},{2,0},{1,3},{3,1},{4,6},{6,4},{5,7},{7,5},{8,10},{10,8},{9,1... | collective-permute-start | bytes 3145736 | tf_op jit(solution)/shard_map/ppermute | solution.py:1102
  178.0 48.5 %all-to-all-start.1 = ((bf16[8,512,128]{2,1,0:T(8,128)(2,1)}), bf16[8,512,128]{2,1,0:T(8,128)(2,1)S(1)}, u32[]{:S(2)}, u32[]{:S(2)}) async-start(bf16[8,512,128]{2,1,0:T(8,128)(2,1)} %get-tuple-element.149.mixed_ref), calls=%async_computation.1 | async-start | bytes 2097152 | tf_op jit(solution)/shard_map/all_to_all | solution.py:1110
  226.5 18.8 %all-to-all-start.2 = ((bf16[8,512,128]{2,1,0:T(8,128)(2,1)}), bf16[8,512,128]{2,1,0:T(8,128)(2,1)S(1)}, u32[]{:S(2)}, u32[]{:S(2)}) async-start(bf16[8,512,128]{2,1,0:T(8,128)(2,1)} %get-tuple-element.146.mixed_ref), calls=%async_computation.2 | async-start | bytes 2097152 | tf_op jit(solution)/shard_map/all_to_all | solution.py:1110
  230.8 102.5 %all-gather.5.cloned.1.call-start = ((), (), s32[]{:S(2)}) async-start(), calls=%async_computation.12 | async-start | bytes 6488064 | tf_op jit(solution)/shard_map/all_gather | solution.py:1208
  333.3 15.0 %collective-permute-start.29 = (bf16[2,2,4,64,4608]{4,3,2,1,0:T(8,128)(2,1)}, bf16[2,2,4,64,4608]{4,3,2,1,0:T(8,128)(2,1)}, u32[]{:S(2)}, u32[]{:S(2)}) collective-permute-start(bf16[2,2,4,64,4608]{4,3,2,1,0:T(8,128)(2,1)} %get-tuple-element.144), channel_id=1, source_target_pairs={{0,2},{2,0},{1,3},{3,1},{4,6},{6,4},{5,7},{7,5},{8,10},{10,8},{9,1... | collective-permute-start | bytes 28311560 | tf_op jit(solution)/shard_map/ppermute | solution.py:1102
  337.3 21.3 %all-to-all-start.4 = ((bf16[8,512,128]{2,1,0:T(8,128)(2,1)}), bf16[8,512,128]{2,1,0:T(8,128)(2,1)S(1)}, u32[]{:S(2)}, u32[]{:S(2)}) async-start(bf16[8,512,128]{2,1,0:T(8,128)(2,1)} %grad_mixed.3), calls=%async_computation.4 | async-start | bytes 2097152 | tf_op jit(solution)/shard_map/all_to_all | solution.py:1110
  340.9 185.7 %reduce-scatter.3.cloned.1.call-start = ((), (), s32[]{:S(2)}) async-start(), calls=%async_computation.13 | async-start | bytes 11796480 | tf_op jit(solution)/shard_map/reduce_scatter | solution.py:1222
  363.6 51.8 %all-to-all-start.3 = ((bf16[8,512,128]{2,1,0:T(8,128)(2,1)}), bf16[8,512,128]{2,1,0:T(8,128)(2,1)S(1)}, u32[]{:S(2)}, u32[]{:S(2)}) async-start(bf16[8,512,128]{2,1,0:T(8,128)(2,1)} %grad_mixed.2), calls=%async_computation.3 | async-start | bytes 2097152 | tf_op jit(solution)/shard_map/all_to_all | solution.py:1110
  416.4 92.8 %all-to-all-start.6 = ((bf16[8,512,384]{2,1,0:T(8,128)(2,1)}), bf16[8,512,384]{2,1,0:T(8,128)(2,1)S(1)}, u32[]{:S(2)}, u32[]{:S(2)}) async-start(bf16[8,512,384]{2,1,0:T(8,128)(2,1)} %attend_back.2.gq_ref), calls=%async_computation.6 | async-start | bytes 6291456 | tf_op jit(solution)/shard_map/all_to_all | solution.py:1110
  504.8 20.0 %collective-permute-start.30 = (bf16[256,384]{1,0:T(8,128)(2,1)}, bf16[256,384]{1,0:T(8,128)(2,1)S(1)}, u32[]{:S(2)}, u32[]{:S(2)}) collective-permute-start(bf16[256,384]{1,0:T(8,128)(2,1)} %get-tuple-element.166), channel_id=1, source_target_pairs={{0,8},{8,0},{16,24},{24,16},{1,9},{9,1},{17,25},{25,17},{2,10},{10... | collective-permute-start | bytes 589832 | tf_op jit(solution)/shard_map/ppermute | solution.py:1102
  504.8 20.0 %collective-permute-start.31 = (bf16[256,384]{1,0:T(8,128)(2,1)}, bf16[256,384]{1,0:T(8,128)(2,1)S(1)}, u32[]{:S(2)}, u32[]{:S(2)}) collective-permute-start(bf16[256,384]{1,0:T(8,128)(2,1)} %get-tuple-element.167), channel_id=1, source_target_pairs={{0,16},{8,24},{16,0},{24,8},{1,17},{9,25},{17,1},{25,9},{2,18},{10... | collective-permute-start | bytes 589832 | tf_op jit(solution)/shard_map/ppermute | solution.py:1102
  504.9 20.0 %collective-permute-start.32 = (bf16[256,384]{1,0:T(8,128)(2,1)}, bf16[256,384]{1,0:T(8,128)(2,1)}, u32[]{:S(2)}, u32[]{:S(2)}) collective-permute-start(bf16[256,384]{1,0:T(8,128)(2,1)} %get-tuple-element.168), channel_id=1, source_target_pairs={{0,24},{8,16},{16,8},{24,0},{1,25},{9,17},{17,9},{25,1},{2,26},{10... | collective-permute-start | bytes 589832 | tf_op jit(solution)/shard_map/ppermute | solution.py:1102
  510.9 41.7 %all-to-all-start.5 = ((bf16[8,512,384]{2,1,0:T(8,128)(2,1)}), bf16[8,512,384]{2,1,0:T(8,128)(2,1)}, u32[]{:S(2)}, u32[]{:S(2)}) async-start(bf16[8,512,384]{2,1,0:T(8,128)(2,1)} %attend_back.3.gq_ref), calls=%async_computation.5 | async-start | bytes 6291456 | tf_op jit(solution)/shard_map/all_to_all | solution.py:1110
  515.5 75.7 %reduce-scatter.5.cloned.1.call-start = ((), (), s32[]{:S(2)}) async-start(), calls=%async_computation.14 | async-start | bytes 2949120 | tf_op jit(solution)/shard_map/reduce_scatter | solution.py:1246
  515.6 9.2 %copy-start.11 = (bf16[256,384]{1,0:T(8,128)(2,1)S(1)}, bf16[256,384]{1,0:T(8,128)(2,1)}, u32[]{:S(2)}) copy-start(bf16[256,384]{1,0:T(8,128)(2,1)} %get-tuple-element.165) | copy-start | bytes 589828
  526.6 35.8 %copy-start.15 = (f32[1,1024]{1,0:T(1,128)S(1)}, f32[1,1024]{1,0:T(1,128)}, u32[]{:S(2)}) copy-start(f32[1,1024]{1,0:T(1,128)} %get-tuple-element.169) | copy-start | bytes 12292
  526.6 39.3 %copy-start.17 = (f32[2,16]{1,0:T(2,128)S(1)}, f32[2,16]{1,0:T(2,128)}, u32[]{:S(2)}) copy-start(f32[2,16]{1,0:T(2,128)} %copy-done.16) | copy-start | bytes 388
  526.6 39.3 %copy-start.19 = (f32[2,16]{1,0:T(2,128)S(1)}, f32[2,16]{1,0:T(2,128)}, u32[]{:S(2)}) copy-start(f32[2,16]{1,0:T(2,128)} %copy-done.18) | copy-start | bytes 388
  526.6 39.3 %copy-start.21 = (f32[2,16]{1,0:T(2,128)S(1)}, f32[2,16]{1,0:T(2,128)}, u32[]{:S(2)}) copy-start(f32[2,16]{1,0:T(2,128)} %copy-done.20) | copy-start | bytes 388
  526.6 39.3 %copy-start.23 = (f32[2,16]{1,0:T(2,128)S(1)}, f32[2,16]{1,0:T(2,128)}, u32[]{:S(2)}) copy-start(f32[2,16]{1,0:T(2,128)} %copy-done.22) | copy-start | bytes 388
  526.6 39.3 %copy-start.6 = (bf16[512,1024]{1,0:T(8,128)(2,1)S(1)}, bf16[512,1024]{1,0:T(8,128)(2,1)}, u32[]{:S(2)}) copy-start(bf16[512,1024]{1,0:T(8,128)(2,1)} %get-tuple-element.160) | copy-start | bytes 3145732
  563.3 17.3 %all-to-all-start.7 = ((bf16[32,4,1024]{2,1,0:T(4,128)(2,1)}), bf16[32,4,1024]{2,1,0:T(4,128)(2,1)S(1)}, u32[]{:S(2)}, u32[]{:S(2)}) async-start(bf16[32,4,1024]{2,1,0:T(4,128)(2,1)} %broadcast_in_dim.26), calls=%async_computation.8 | async-start | bytes 524288 | tf_op jit(solution)/shard_map/all_to_all | solution.py:1110
  580.6 8.7 %all-to-all-start.8 = ((bf16[4,64,384]{2,1,0:T(8,128)(2,1)}), bf16[4,64,384]{2,1,0:T(8,128)(2,1)S(1)}, u32[]{:S(2)}, u32[]{:S(2)}) async-start(bf16[4,64,384]{2,1,0:T(8,128)(2,1)} %bitcast.26), calls=%async_computation.9 | async-start | bytes 393216 | tf_op jit(solution)/shard_map/all_to_all | solution.py:1110
  (10 other events, 18.9 us)
Sparse Core Ops, SparseCore 0:
  39.6 147.7 all-gather.2
  251.3 66.7 all-gather.4
  358.8 133.6 reduce-scatter.2
  526.7 50.0 reduce-scatter.4
